TPU v7x, 32 devices: a whole 2x2x4 slice. The times are simulated.
32 devices in a mesh: lead: 2 (over x), tile: 16 (over z, y, core).
Axes of the slice: x: 2, y: 2, z: 4, core: 2. Of those that a mesh axis runs over, the one named last changes fastest.
Arguments:
- states: float32 [2, 2, 128, 128, 128], P('lead', None, None, 'tile'), may hold values from -6 to 6
- cotangents: float32 [2, 2, 128, 128, 128], P('lead', None, None, 'tile'), may hold values from -6 to 6
- w_conv: bfloat16 [1152, 512], replicated, may hold values from -0.1875 to 0.1875
- b_conv: float32 [512], replicated, may hold values from -3 to 3
- w_out: bfloat16 [512, 128], replicated, may hold values from -0.25 to 0.25
- forcing: float32 [365, 128], replicated, may hold values from -3 to 3
- land: int32 [128, 128], P('tile'), may hold values 0 or 1
- dates: int32 [2], replicated, may hold values from 0 to 364
Outputs:
- state_grads: float32 [2, 2, 128, 128, 128], P('lead', None, None, 'tile')
- w1_grad: float32 [1152, 512], P('tile')
- w2_grad: float32 [512, 128], P('tile')
- b1_grad: float32 [512], P('tile')
Inputs may be any that keep to these rules, and one draw needn't show every extreme that they name: 1 marks an ocean column, 0 a land column.
All inputs are finite; a program needn't handle non-finite values. No bound on the sum of `land` on one device may be relied on, other than what follows from the above.
Results may differ from a plain program's by a relative error of at most 0.0056.
Values may be sent and summed in bfloat16 or wider, within the bound.
No kernel may reach another device: no remote copies, remote signals or barrier semaphores. Data moves between devices by JAX's collectives and lax.ppermute only.
A program may use at most 128 MiB of HBM per device.

v0:
```python
import functools
import math

import jax
import jax.numpy as jnp
from jax import lax
from jax.experimental import pallas as pl
from jax.experimental.pallas import tpu as pltpu
from jax.sharding import PartitionSpec as P

TANH_SCALE = 0.7978845608028654
CUBIC_TERM = 0.044715
BF16 = jnp.bfloat16
F32 = jnp.float32
PARAMS = pltpu.CompilerParams(vmem_limit_bytes=32 * 1024 * 1024)


def dot(left, right):
    return jnp.dot(left, right, preferred_element_type=F32)


def dot_t(left, right):
    return lax.dot_general(left, right, (((1,), (1,)), ((), ())), preferred_element_type=F32)


def gelu_pair(v):
    square = v * v
    t = jnp.tanh(TANH_SCALE * (v + CUBIC_TERM * (square * v)))
    half = 0.5 * (1.0 + t)
    slope = half + (0.5 * v) * (1.0 - t * t) * (TANH_SCALE * (1.0 + 3.0 * CUBIC_TERM * square))
    return v * half, slope


def member_block(shape, member):
    rest = len(shape) - 1
    return pl.BlockSpec((1,) + tuple(shape[1:]), lambda i: (member,) + (0,) * rest)


def full_block(shape):
    return pl.BlockSpec(tuple(shape), lambda i: (0,) * len(shape))


def prep_body(rows, dates, section, forcing, states, cot, land, rounded, top, bottom):
    m = pl.program_id(0)
    days, channels = forcing.shape
    lon = states.shape[2]
    day = (dates[m] + section[0]) % days
    line = forcing[pl.ds(day, 1), :]
    shift = jnp.broadcast_to(line, (lon, channels)).T
    for r in range(rows):
        value = (states[0, pl.ds(r, channels, stride=rows), :] + shift).astype(BF16)
        rounded[0, r] = value
        if r < 2:
            top[0, r] = value
        if r >= rows - 2:
            bottom[0, r - (rows - 2)] = value
    top[0, 2] = masked_row(0, channels, cot, land, total_row(0, rows, channels, cot, 0))
    bottom[0, 2] = masked_row(rows - 1, channels, cot, land, total_row(rows - 1, rows, channels, cot, 0))


def prep(dates, section, forcing, states, cot, land):
    members, flat, lon = states.shape
    rows = land.shape[0]
    channels = flat // rows
    smem = pl.BlockSpec(memory_space=pltpu.SMEM)
    own = pl.BlockSpec((1, flat, lon), lambda m: (m, 0, 0))
    halo = pl.BlockSpec((1, 3, channels, lon), lambda m: (m, 0, 0, 0))
    return pl.pallas_call(
        functools.partial(prep_body, rows),
        grid=(members,),
        in_specs=[smem, smem, full_block(forcing.shape), own, own, full_block(land.shape)],
        out_specs=[pl.BlockSpec((1, rows, channels, lon), lambda m: (m, 0, 0, 0)), halo, halo],
        out_shape=[
            jax.ShapeDtypeStruct((members, rows, channels, lon), BF16),
            jax.ShapeDtypeStruct((members, 3, channels, lon), BF16),
            jax.ShapeDtypeStruct((members, 3, channels, lon), BF16),
        ],
        name="prep",
    )(dates, section, forcing, states, cot, land)


def turn_body(w_conv, b_conv, turned, column):
    turned[...] = w_conv[...].T
    column[...] = jnp.broadcast_to(b_conv[...], (column.shape[1], column.shape[0])).T


def turn(w_conv, b_conv, lanes):
    taps, hidden = w_conv.shape
    return pl.pallas_call(
        turn_body,
        out_shape=[
            jax.ShapeDtypeStruct((hidden, taps), BF16),
            jax.ShapeDtypeStruct((hidden, lanes), F32),
        ],
        compiler_params=PARAMS,
        name="turn",
    )(w_conv, b_conv)


def edge_grads(w_conv, pre, channels, rows, lon):
    out = []
    for rs, source in ((0, 0), (2, rows - 1)):
        block = w_conv[rs * 3 * channels : (rs + 1) * 3 * channels, :]
        part = dot(block, pre[:, source * lon : (source + 1) * lon])
        out.append(
            part[channels : 2 * channels]
            + pltpu.roll(part[:channels], lon - 1, 1)
            + pltpu.roll(part[2 * channels :], 1, 1)
        )
    return out


def own_grads(w_conv, pre, z, channels, rows, lon, halo):
    taps = 9 * channels
    for k in range(0, rows, 2):
        cols = slice((k + halo) * lon, (k + halo + 2) * lon)
        z[0:taps, cols] = dot(w_conv[...], pre[:, cols])
    for source, rs in ((-1, 2), (rows, 0)) if halo else ():
        cols = slice((source + 1) * lon, (source + 2) * lon)
        block = slice(rs * 3 * channels, (rs + 1) * 3 * channels)
        z[block, cols] = dot(w_conv[block, :], pre[:, cols])
    for i in range(rows):
        per_step = []
        for cs in range(3):
            total = None
            for rs in range(3):
                source = i - (rs - 1)
                if -halo <= source < rows + halo:
                    tap = 3 * rs + cs
                    at = (source + halo) * lon
                    term = z[tap * channels : (tap + 1) * channels, at : at + lon]
                    total = term if total is None else total + term
            per_step.append(total)
        yield per_step[1] + pltpu.roll(per_step[0], lon - 1, 1) + pltpu.roll(per_step[2], 1, 1)


def total_row(r, rows, channels, cot, member, main=None):
    total = cot[member, pl.ds(r, channels, stride=rows), :]
    return total if main is None else total + main[r].astype(F32)


def masked_row(r, channels, cot, land, total):
    return (land[r : r + 1, :].astype(F32) * total).astype(BF16)


def build_stack(rounded, low, high, stack, member, halo):
    _, rows, channels, lon = rounded.shape
    for q in range(-halo, rows + halo):
        if q < 0:
            x = low[member, 2 + q]
        elif q >= rows:
            x = high[member, q - rows]
        else:
            x = rounded[member, q]
        wide = x.astype(F32)
        at = slice((q + halo) * lon, (q + halo + 1) * lon)
        stack[0:channels, at] = pltpu.roll(wide, 1, 1).astype(BF16)
        stack[channels : 2 * channels, at] = x
        stack[2 * channels : 3 * channels, at] = pltpu.roll(wide, lon - 1, 1).astype(BF16)


def forward_body(
    rounded, low, high, turned, column, w_conv, w_out, cot, land,
    main, hidden_out, slope_out, stack, hidden, slope, masked, pre, z, sems,
):
    _, rows, channels, lon = rounded.shape
    build_stack(rounded, low, high, stack, 0, 2)
    masked[:, 0:lon] = low[0, 2]
    for r in range(rows):
        masked[:, (r + 1) * lon : (r + 2) * lon] = masked_row(
            r, channels, cot, land, total_row(r, rows, channels, cot, 0)
        )
    masked[:, (rows + 1) * lon :] = high[0, 2]
    bias = jnp.concatenate([column[...], column[...]], axis=1)
    for k in range(0, rows + 2, 2):
        preact = bias
        for rs in range(3):
            preact = preact + dot(
                turned[:, rs * 3 * channels : (rs + 1) * 3 * channels],
                stack[:, (k + rs) * lon : (k + rs + 2) * lon],
            )
        value, steep = gelu_pair(preact)
        cols = slice(k * lon, (k + 2) * lon)
        hidden[:, cols] = value.astype(BF16)
        slope[:, cols] = steep
        pre[:, cols] = (dot(w_out[...], masked[:, cols]) * steep).astype(BF16)
    inner = slice(lon, (rows + 1) * lon)
    copies = [
        pltpu.make_async_copy(hidden.at[:, inner], hidden_out, sems.at[0]),
        pltpu.make_async_copy(slope.at[:, inner], slope_out, sems.at[1]),
    ]
    for copy in copies:
        copy.start()
    for r, grad in enumerate(own_grads(w_conv, pre, z, channels, rows, lon, 1)):
        main[r] = (grad + total_row(r, rows, channels, cot, 0)).astype(BF16)
    for copy in copies:
        copy.wait()


def forward(member, rounded, low, high, turned, column, w_conv, w_out, cot, land):
    _, rows, channels, lon = rounded.shape
    taps, width = w_conv.shape
    cols, more = rows * lon, (rows + 2) * lon
    operands = [rounded, low, high, turned, column, w_conv, w_out, cot, land]
    specs = [member_block(x.shape, member) for x in (rounded, low, high)]
    specs += [full_block(x.shape) for x in (turned, column, w_conv, w_out)]
    specs += [member_block(cot.shape, member), full_block(land.shape)]
    main = (rows, channels, lon)
    hbm = pl.BlockSpec(memory_space=pltpu.HBM)
    return pl.pallas_call(
        forward_body,
        grid=(1,),
        in_specs=specs,
        out_specs=[full_block(main), hbm, hbm],
        out_shape=[jax.ShapeDtypeStruct(main, BF16), pltpu.HBM((width, cols), BF16), pltpu.HBM((width, cols), F32)],
        scratch_shapes=[
            pltpu.VMEM((3 * channels, (rows + 4) * lon), BF16),
            pltpu.VMEM((width, more), BF16),
            pltpu.VMEM((width, more), F32),
            pltpu.VMEM((channels, more), BF16),
            pltpu.VMEM((width, more), BF16),
            pltpu.VMEM((taps, more), F32),
            pltpu.SemaphoreType.DMA((2,)),
        ],
        compiler_params=PARAMS,
        name=f"forward_{member}",
    )(*operands)


def phase_bits(parts, core):
    bits = list(range(parts.bit_length() - 1))
    if len(bits) > 2 and core == 1:
        bits[1], bits[2] = bits[2], bits[1]
    return bits


def place_of(relative, core, parts):
    even, odd = phase_bits(parts, 0), phase_bits(parts, 1)
    depth = len(even)
    place = 0
    for i in range(1, depth):
        bit = (relative >> even[i]) & 1
        if even[i] != odd[i]:
            bit = jnp.where(core == 0, bit, (relative >> odd[i]) & 1)
        place = place + (bit << (depth - 1 - i))
    return place


def weight_body(members, parts, here_ref, rounded, low, high, cot, land, w_out, w_conv, *refs):
    mains, held = refs[:members], refs[members : 3 * members]
    give, keep, up, down = refs[3 * members : 3 * members + 4]
    pres = refs[3 * members + 4 : 4 * members + 4]
    refs = refs[4 * members + 4 :]
    local = refs[: 2 * members]
    stack, masked, w1, w2, sems = refs[2 * members :]
    _, rows, channels, lon = rounded.shape
    width = w_out.shape[0]
    cols = rows * lon
    copies = [pltpu.make_async_copy(a, b, sems.at[i]) for i, (a, b) in enumerate(zip(held, local))]
    for copy in copies:
        copy.start()
    acc = None
    for m in range(members):
        hidden, slope = local[2 * m : 2 * m + 2]
        build_stack(rounded, low, high, stack.at[m], m, 1)
        for r in range(rows):
            masked[m, :, r * lon : (r + 1) * lon] = masked_row(
                r, channels, cot, land, total_row(r, rows, channels, cot, m, mains[m])
            )
        copies[2 * m].wait()
        part = dot_t(hidden[...], masked[m])
        w2[...] = part if m == 0 else part + w2[...]
        copies[2 * m + 1].wait()
        for k in range(0, rows, 2):
            at = slice(k * lon, (k + 2) * lon)
            grad = dot(w_out[...], masked[m, :, at]) * slope[:, at]
            pres[m][:, at] = grad.astype(BF16)
            both = grad[:, :lon] + grad[:, lon:]
            acc = both if acc is None else acc + both
        above, below = edge_grads(w_conv, pres[m], channels, rows, lon)
        up[m] = above.astype(BF16)
        down[m] = below.astype(BF16)
        for rs in range(3):
            at = slice(rs * 3 * channels, (rs + 1) * 3 * channels)
            part = dot_t(stack[m, :, rs * lon : rs * lon + cols], pres[m][...])
            w1[at, :] = part if m == 0 else part + w1[at, :]

    here = here_ref[0]
    core = here & 1
    line = jnp.sum(acc.T, axis=0, keepdims=True)
    deep, wide = w1.shape[0] // parts, width // parts
    folds = width // channels
    thin = wide // folds

    def fill(target, place, t):
        kind = target.dtype
        target[place, 0:deep, :] = w1[t * deep : (t + 1) * deep, :].astype(kind)
        for f in range(folds):
            target[place, deep : deep + thin, f * channels : (f + 1) * channels] = w2[
                t * wide + f * thin : t * wide + (f + 1) * thin, :
            ].astype(kind)
        shifted = line if t == 0 else pltpu.roll(line, width - t * wide, 1)
        target[place, deep + thin : deep + thin + 1, :] = shifted.astype(kind)

    for t in range(parts):
        relative = here ^ t

        @pl.when((relative & 1) == 0)
        def _():
            fill(keep, place_of(relative, core, parts), t)

        @pl.when((relative & 1) == 1)
        def _():
            fill(give, place_of(relative, 1 - core, parts), t)


def packed_rows(taps, width, channels, parts):
    used = taps // parts + width // parts // (width // channels) + 1
    return -(-used // 8) * 8


def weight(here, parts, rounded, low, high, cot, land, w_out, w_conv, mains, kept):
    members, rows, channels, lon = rounded.shape
    taps, width = w_conv.shape
    cols = rows * lon

    def full(shape):
        return pl.BlockSpec(tuple(shape), lambda i, _: (0,) * len(shape))

    operands = [rounded, low, high, cot, land, w_out, w_conv, *mains]
    specs = [full(x.shape) for x in operands]
    held = [x for row in kept for x in row]
    operands += [pltpu.with_memory_space_constraint(x, pltpu.HBM) for x in held]
    specs += [pl.BlockSpec(memory_space=pltpu.HBM) for _ in held]
    chunk = (parts // 2, packed_rows(taps, width, channels, parts), width)
    edge = (members, channels, lon)
    shapes = [(chunk, BF16), (chunk, F32), (edge, BF16), (edge, BF16)] + [((width, cols), BF16)] * members
    return pl.pallas_call(
        functools.partial(weight_body, members, parts),
        grid_spec=pltpu.PrefetchScalarGridSpec(
            num_scalar_prefetch=1,
            grid=(1,),
            in_specs=specs,
            out_specs=[full(s) for s, _ in shapes],
            scratch_shapes=[pltpu.VMEM(x.shape, x.dtype) for x in held]
            + [
                pltpu.VMEM((members, 3 * channels, (rows + 2) * lon), BF16),
                pltpu.VMEM((members, channels, cols), BF16),
                pltpu.VMEM((taps, width), F32),
                pltpu.VMEM((width, channels), F32),
                pltpu.SemaphoreType.DMA((len(held),)),
            ],
        ),
        out_shape=[jax.ShapeDtypeStruct(s, d) for s, d in shapes],
        compiler_params=PARAMS,
        name="weight",
    )(here, *operands)


def state_body(members, w_conv, cot, beside_low, beside_high, *refs):
    pres, mains = refs[:members], refs[members : 2 * members]
    out, z = refs[2 * members :]
    rows, channels, lon = mains[0].shape
    for m in range(members):
        for r, grad in enumerate(own_grads(w_conv, pres[m], z.at[m % 2], channels, rows, lon, 0)):
            total = grad + total_row(r, rows, channels, cot, m, mains[m])
            if r == 0:
                total = total + beside_low[m].astype(F32)
            if r == rows - 1:
                total = total + beside_high[m].astype(F32)
            out[m, pl.ds(r, channels, stride=rows), :] = total


def state_grad(w_conv, cot, beside_low, beside_high, pres, mains):
    taps = w_conv.shape[0]
    operands = [w_conv, cot, beside_low, beside_high, *pres, *mains]
    return pl.pallas_call(
        functools.partial(state_body, len(pres)),
        grid=(1,),
        in_specs=[full_block(x.shape) for x in operands],
        out_specs=full_block(cot.shape),
        out_shape=jax.ShapeDtypeStruct(cot.shape, F32),
        scratch_shapes=[pltpu.VMEM((2, taps, pres[0].shape[1]), F32)],
        compiler_params=PARAMS,
        name="state",
    )(*operands)


def finish_body(scale, own, taken, w1, w2, b1):
    deep = w1.shape[0]
    wide, channels = w2.shape
    folds = own.shape[2] // channels
    thin = wide // folds
    total = (own[0] + taken[0].astype(F32)) * scale
    w1[...] = total[:deep]
    for f in range(folds):
        w2[f * thin : (f + 1) * thin, :] = total[deep : deep + thin, f * channels : (f + 1) * channels]
    b1[...] = total[deep + thin : deep + thin + 1, :wide]


def finish(scale, own, taken, deep, wide, channels):
    return pl.pallas_call(
        functools.partial(finish_body, scale),
        out_shape=[
            jax.ShapeDtypeStruct((deep, own.shape[2]), F32),
            jax.ShapeDtypeStruct((wide, channels), F32),
            jax.ShapeDtypeStruct((1, wide), F32),
        ],
        compiler_params=PARAMS,
        name="finish",
    )(own, taken)


def shards(states, cotangents, w_conv, b_conv, w_out, forcing, land, dates):
    section = lax.axis_index("lead").astype(jnp.int32)
    here = lax.axis_index("tile").astype(jnp.int32)
    leads = lax.axis_size("lead")
    tiles = lax.axis_size("tile")
    _, members, channels, rows, lon = states.shape
    taps, width = w_conv.shape
    own = states.reshape(members, channels * rows, lon)
    cot = cotangents.reshape(members, channels * rows, lon)
    rounded, top, bottom = prep(dates, section[None], forcing, own, cot, land)
    ahead = [(t, t + 1) for t in range(tiles - 1)]
    behind = [(t + 1, t) for t in range(tiles - 1)]
    low = lax.ppermute(bottom, "tile", ahead)
    high = lax.ppermute(top, "tile", behind)
    turned, column = turn(w_conv, b_conv[None, :], lon)

    steps = [(s, s - 1) for s in range(1, leads)]
    kept = []
    mains = []
    for m in range(members):
        main, hidden, slope = forward(m, rounded, low, high, turned, column, w_conv, w_out, cot, land)
        kept.append((hidden, slope))
        mains.append(lax.ppermute(main, "lead", steps))
    give, keep, up, down, *pres = weight(
        here[None], tiles, rounded, low, high, cot, land, w_out, w_conv, mains, kept
    )

    assert tiles >= 8

    def exchanged(value, step):
        bits = (phase_bits(tiles, 0)[step], phase_bits(tiles, 1)[step])
        return lax.ppermute(value, "tile", [(t, t ^ (1 << bits[t & 1])) for t in range(tiles)])

    depth = tiles.bit_length() - 1
    total = keep + exchanged(give, 0).astype(F32)
    for step in range(1, depth):
        half = total.shape[0] // 2
        send = total[half:].astype(BF16)
        if step == 1:
            send, up, down = lax.optimization_barrier((send, up, down))
            beside_low = lax.ppermute(down, "tile", ahead)
            beside_high = lax.ppermute(up, "tile", behind)
        if step == 2:
            send, beside_low, beside_high = lax.optimization_barrier((send, beside_low, beside_high))
            body = state_grad(w_conv, cot, beside_low, beside_high, pres, mains)
        taken = exchanged(send, step)
        if step == 1:
            taken, beside_low, beside_high = lax.optimization_barrier((taken, beside_low, beside_high))
        if step == 2:
            taken, body = lax.optimization_barrier((taken, body))
        total = total[:half] + taken.astype(F32)
    grads = body.reshape(states.shape)
    taken = lax.ppermute(total.astype(BF16), "lead", [(s, leads - 1 - s) for s in range(leads)])
    scale = 1.0 / math.sqrt(leads * members * rows * tiles * lon)
    w1, w2, b1 = finish(scale, total, taken, taps // tiles, width // tiles, channels)
    return grads, w1, w2, b1[0]


def solution(mesh):
    assert mesh.shape["lead"] == 2
    placed = (
        P("lead", None, None, "tile", None),
        P("lead", None, None, "tile", None),
        P(),
        P(),
        P(),
        P(),
        P("tile", None),
        P(),
    )
    return jax.shard_map(
        shards,
        mesh=mesh,
        in_specs=placed,
        out_specs=(
            P("lead", None, None, "tile", None),
            P("tile", None),
            P("tile", None),
            P("tile"),
        ),
        check_vma=False,
    )
```

profile of v0, /device:TPU:0, one launch (start us, length us, event | category | flops | bytes accessed | tf_op | source)
XLA Modules:
  0.0 81.1 jit_solution(979982636586181535)
XLA Ops:
  0.7 2.7 %prep.1 = (bf16[2,8,128,128]{3,2,1,0:T(8,128)(2,1)}, bf16[2,3,128,128]{3,2,1,0:T(8,128)(2,1)}, bf16[2,3,128,128]{3,2,1,0:T(8,128)(2,1)}) custom-call(s32[2]{0:T(128)} %dates.1, s32[1]{0:T(128)} %bitcast.1.section, f32[365,128]{1,0:T(8,128)} %forcing.1, f32[2,1024,128]{2,1,0:T(8,128)} %bitcast.13, f32[2,1024,128]{2,1,0:T(8,128)} %bitcast.7, s32[8,128]{1,0:T(8,128)} %land.7), custom_call_target="tpu_custom_call" | custom-call | tf_op jit(solution)/shard_map/prep/pallas_call | solution.py:68
  3.4 2.5 %collective-permute-start = (bf16[2,3,128,128]{3,2,1,0:T(8,128)(2,1)}, bf16[2,3,128,128]{3,2,1,0:T(8,128)(2,1)S(1)}, u32[]{:S(2)}, u32[]{:S(2)}) collective-permute-start(bf16[2,3,128,128]{3,2,1,0:T(8,128)(2,1)} %get-tuple-element.36), channel_id=1, source_target_pairs={{0,1},{1,2},{2,3},{3,4},{4,5},{5,6},{6,7},{7,8},{8,9},{9,10},{10,1... | collective-permute-start | bytes 589832 | tf_op jit(solution)/shard_map/ppermute | solution.py:426
  6.0 1.3 %collective-permute-start.1 = (bf16[2,3,128,128]{3,2,1,0:T(8,128)(2,1)}, bf16[2,3,128,128]{3,2,1,0:T(8,128)(2,1)S(1)}, u32[]{:S(2)}, u32[]{:S(2)}) collective-permute-start(bf16[2,3,128,128]{3,2,1,0:T(8,128)(2,1)} %get-tuple-element.37), channel_id=1, source_target_pairs={{1,0},{2,1},{3,2},{4,3},{5,4},{6,5},{7,6},{8,7},{9,8},{10,9},{11,1... | collective-permute-start | bytes 589832 | tf_op jit(solution)/shard_map/ppermute | solution.py:427
  7.3 0.4 turn.1
  7.7 0.0 collective-permute-done.low
  7.8 3.9 %collective-permute-done.1.high = bf16[2,3,128,128]{3,2,1,0:T(8,128)(2,1)S(1)} collective-permute-done((bf16[2,3,128,128]{3,2,1,0:T(8,128)(2,1)}, bf16[2,3,128,128]{3,2,1,0:T(8,128)(2,1)S(1)}, u32[]{:S(2)}, u32[]{:S(2)}) %collective-permute-start.1) | collective-permute-done | bytes 196640 | tf_op jit(solution)/shard_map/ppermute | solution.py:427
  11.6 0.0 copy-done.1
  11.7 6.5 %forward_1.1 = (bf16[8,128,128]{2,1,0:T(8,128)(2,1)}, bf16[512,1024]{1,0:T(8,128)(2,1)}, f32[512,1024]{1,0:T(8,128)}) custom-call(bf16[2,8,128,128]{3,2,1,0:T(8,128)(2,1)S(1)} %copy-done.2, bf16[2,3,128,128]{3,2,1,0:T(8,128)(2,1)S(1)} %collective-permute-done.low, bf16[2,3,128,128]{3,2,1,0:T(8,128)(2,1)S(1)} %collective-permute-done.1.high, ...), custom_call_target="tpu_custom_call" | custom-call | tf_op jit(solution)/shard_map/forward_1/pallas_call | solution.py:210
  18.2 1.3 %collective-permute-start.3 = (bf16[8,128,128]{2,1,0:T(8,128)(2,1)}, bf16[8,128,128]{2,1,0:T(8,128)(2,1)S(1)}, u32[]{:S(2)}, u32[]{:S(2)}) collective-permute-start(bf16[8,128,128]{2,1,0:T(8,128)(2,1)} %get-tuple-element.41), channel_id=1, source_target_pairs={{16,0},{17,1},{18,2},{19,3},{20,4},{21,5},{22,6},{23,7},{24,8},{25... | collective-permute-start | bytes 786440 | tf_op jit(solution)/shard_map/ppermute | solution.py:436
  19.5 6.5 %forward_0.1 = (bf16[8,128,128]{2,1,0:T(8,128)(2,1)}, bf16[512,1024]{1,0:T(8,128)(2,1)}, f32[512,1024]{1,0:T(8,128)}) custom-call(bf16[2,8,128,128]{3,2,1,0:T(8,128)(2,1)S(1)} %copy-done.2, bf16[2,3,128,128]{3,2,1,0:T(8,128)(2,1)S(1)} %collective-permute-done.low, bf16[2,3,128,128]{3,2,1,0:T(8,128)(2,1)S(1)} %collective-permute-done.1.high, ...), custom_call_target="tpu_custom_call" | custom-call | tf_op jit(solution)/shard_map/forward_0/pallas_call | solution.py:210
  26.1 1.5 %collective-permute-start.2 = (bf16[8,128,128]{2,1,0:T(8,128)(2,1)}, bf16[8,128,128]{2,1,0:T(8,128)(2,1)}, u32[]{:S(2)}, u32[]{:S(2)}) collective-permute-start(bf16[8,128,128]{2,1,0:T(8,128)(2,1)} %get-tuple-element.40), channel_id=1, source_target_pairs={{16,0},{17,1},{18,2},{19,3},{20,4},{21,5},{22,6},{23,7},{24,8},{25... | collective-permute-start | bytes 786440 | tf_op jit(solution)/shard_map/ppermute | solution.py:436
  27.5 0.0 collective-permute-done.3.refs_1_.refs_3_
  27.6 7.1 %collective-permute-done.2.refs_0_.refs_2_ = bf16[8,128,128]{2,1,0:T(8,128)(2,1)} collective-permute-done((bf16[8,128,128]{2,1,0:T(8,128)(2,1)}, bf16[8,128,128]{2,1,0:T(8,128)(2,1)}, u32[]{:S(2)}, u32[]{:S(2)}) %collective-permute-start.2) | collective-permute-done | bytes 262176 | tf_op jit(solution)/shard_map/ppermute | solution.py:436
  34.7 9.2 %weight.1 = (bf16[8,88,512]{2,1,0:T(8,128)(2,1)S(1)}, f32[8,88,512]{2,1,0:T(8,128)S(1)}, bf16[2,128,128]{2,1,0:T(8,128)(2,1)S(1)}, bf16[2,128,128]{2,1,0:T(8,128...) custom-call(s32[1]{0:T(128)} %bitcast.here_ref, bf16[2,8,128,128]{3,2,1,0:T(8,128)(2,1)S(1)} %copy-done.2, ...), custom_call_target="tpu_custom_call" | custom-call | tf_op jit(solution)/shard_map/weight/pallas_call | solution.py:338
  43.8 3.0 %collective-permute-start.4 = (bf16[8,88,512]{2,1,0:T(8,128)(2,1)S(1)}, bf16[8,88,512]{2,1,0:T(8,128)(2,1)S(1)}, u32[]{:S(2)}, u32[]{:S(2)}) collective-permute-start(bf16[8,88,512]{2,1,0:T(8,128)(2,1)S(1)} %get-tuple-element.47), channel_id=1, source_target_pairs={{0,1},{1,0},{2,3},{3,2},{4,5},{5,4},{6,7},{7,6},{8,9},{9,8},{10,11... | collective-permute-start | bytes 2162696 | tf_op jit(solution)/shard_map/ppermute | solution.py:445
  46.9 1.8 %collective-permute-done.4 = bf16[8,88,512]{2,1,0:T(8,128)(2,1)S(1)} collective-permute-done((bf16[8,88,512]{2,1,0:T(8,128)(2,1)S(1)}, bf16[8,88,512]{2,1,0:T(8,128)(2,1)S(1)}, u32[]{:S(2)}, u32[]{:S(2)}) %collective-permute-start.4) | collective-permute-done | bytes 720928 | tf_op jit(solution)/shard_map/ppermute | solution.py:445
  48.7 0.2 convert_add_fusion
  49.0 3.7 %collective-permute-start.5 = (bf16[4,88,512]{2,1,0:T(8,128)(2,1)S(1)}, bf16[4,88,512]{2,1,0:T(8,128)(2,1)S(1)}, u32[]{:S(2)}, u32[]{:S(2)}) collective-permute-start(bf16[4,88,512]{2,1,0:T(8,128)(2,1)S(1)} %slice.39), channel_id=1, source_target_pairs={{0,2},{1,5},{2,0},{3,7},{4,6},{5,1},{6,4},{7,3},{8,10},{9,13},{10,... | collective-permute-start | bytes 1081352 | tf_op jit(solution)/shard_map/ppermute | solution.py:445
  52.6 3.1 %collective-permute-start.6 = (bf16[2,128,128]{2,1,0:T(8,128)(2,1)S(1)}, bf16[2,128,128]{2,1,0:T(8,128)(2,1)S(1)}, u32[]{:S(2)}, u32[]{:S(2)}) collective-permute-start(bf16[2,128,128]{2,1,0:T(8,128)(2,1)S(1)} %get-tuple-element.51), channel_id=1, source_target_pairs={{0,1},{1,2},{2,3},{3,4},{4,5},{5,6},{6,7},{7,8},{8,9},{9,10},{10,1... | collective-permute-start | bytes 196616 | tf_op jit(solution)/shard_map/ppermute | solution.py:454
  55.8 1.3 %collective-permute-start.7 = (bf16[2,128,128]{2,1,0:T(8,128)(2,1)S(1)}, bf16[2,128,128]{2,1,0:T(8,128)(2,1)S(1)}, u32[]{:S(2)}, u32[]{:S(2)}) collective-permute-start(bf16[2,128,128]{2,1,0:T(8,128)(2,1)S(1)} %get-tuple-element.52), channel_id=1, source_target_pairs={{1,0},{2,1},{3,2},{4,3},{5,4},{6,5},{7,6},{8,7},{9,8},{10,9},{11,1... | collective-permute-start | bytes 196616 | tf_op jit(solution)/shard_map/ppermute | solution.py:455
  57.1 0.0 collective-permute-done.6.beside_low
  57.1 1.8 %collective-permute-done.7.beside_high = bf16[2,128,128]{2,1,0:T(8,128)(2,1)S(1)} collective-permute-done((bf16[2,128,128]{2,1,0:T(8,128)(2,1)S(1)}, bf16[2,128,128]{2,1,0:T(8,128)(2,1)S(1)}, u32[]{:S(2)}, u32[]{:S(2)}) %collective-permute-start.7) | collective-permute-done | bytes 65568 | tf_op jit(solution)/shard_map/ppermute | solution.py:455
  58.9 0.0 collective-permute-done.5
  58.9 0.1 slice_add_fusion
  59.1 3.7 %collective-permute-start.8 = (bf16[2,88,512]{2,1,0:T(8,128)(2,1)S(1)}, bf16[2,88,512]{2,1,0:T(8,128)(2,1)S(1)}, u32[]{:S(2)}, u32[]{:S(2)}) collective-permute-start(bf16[2,88,512]{2,1,0:T(8,128)(2,1)S(1)} %slice.40), channel_id=1, source_target_pairs={{0,4},{1,3},{2,6},{3,1},{4,0},{5,7},{6,2},{7,5},{8,12},{9,11},{10,... | collective-permute-start | bytes 540680 | tf_op jit(solution)/shard_map/ppermute | solution.py:445
  62.8 4.7 %state.1 = f32[2,1024,128]{2,1,0:T(8,128)} custom-call(bf16[1152,512]{1,0:T(8,128)(2,1)S(1)} %copy-done, f32[2,1024,128]{2,1,0:T(8,128)S(1)} %bitcast.11, bf16[2,128,128]{2,1,0:T(8,128)(2,1)S(1)} %collective-permute-done.6.beside_low, bf16[2,128,128]{2,1,0:T(8,128)(2,1)S(1)} %collective-permute-done.7.beside_high, ...), custom_call_target="tpu_custom_call" | custom-call | tf_op jit(solution)/shard_map/state/pallas_call | solution.py:377
  67.5 0.0 collective-permute-done.8
  67.6 2.5 %collective-permute-start.9 = (bf16[1,88,512]{2,1,0:T(8,128)(2,1)S(1)}, bf16[1,88,512]{2,1,0:T(8,128)(2,1)S(1)}, u32[]{:S(2)}, u32[]{:S(2)}) collective-permute-start(bf16[1,88,512]{2,1,0:T(8,128)(2,1)S(1)} %slice.41), channel_id=1, source_target_pairs={{0,8},{1,9},{2,10},{3,11},{4,12},{5,13},{6,14},{7,15},{8,0},{9,1},... | collective-permute-start | bytes 270344 | tf_op jit(solution)/shard_map/ppermute | solution.py:445
  70.0 5.6 %collective-permute-done.9 = bf16[1,88,512]{2,1,0:T(8,128)(2,1)S(1)} collective-permute-done((bf16[1,88,512]{2,1,0:T(8,128)(2,1)S(1)}, bf16[1,88,512]{2,1,0:T(8,128)(2,1)S(1)}, u32[]{:S(2)}, u32[]{:S(2)}) %collective-permute-start.9) | collective-permute-done | bytes 90144 | tf_op jit(solution)/shard_map/ppermute | solution.py:445
  75.6 0.1 collective-permute-start.10
  75.7 4.7 %collective-permute-done.10.taken = bf16[1,88,512]{2,1,0:T(8,128)(2,1)S(1)} collective-permute-done((bf16[1,88,512]{2,1,0:T(8,128)(2,1)S(1)}, bf16[1,88,512]{2,1,0:T(8,128)(2,1)S(1)}, u32[]{:S(2)}, u32[]{:S(2)}) %collective-permute-start.10) | collective-permute-done | bytes 90144 | tf_op jit(solution)/shard_map/ppermute | solution.py:466
  80.4 0.7 finish.1
  (16 shorter events, 0.2 us)
Async XLA Ops:
  0.6 6.6 %copy-start = (bf16[1152,512]{1,0:T(8,128)(2,1)S(1)}, bf16[1152,512]{1,0:T(8,128)(2,1)}, u32[]{:S(2)}) copy-start(bf16[1152,512]{1,0:T(8,128)(2,1)} %w_conv.9) | copy-start | bytes 3538948
  0.6 6.6 %copy-start.5 = (f32[512]{0:T(512)S(1)}, f32[512]{0:T(512)}, u32[]{:S(2)}) copy-start(f32[512]{0:T(512)} %param.11) | copy-start | bytes 6148
  0.7 11.0 %copy-start.1 = (f32[1,2,128,8,128]{4,3,2,1,0:T(8,128)S(1)}, f32[1,2,128,8,128]{4,3,2,1,0:T(8,128)}, u32[]{:S(2)}) copy-start(f32[1,2,128,8,128]{4,3,2,1,0:T(8,128)} %param.9) | copy-start | bytes 3145732
  0.7 11.0 %copy-start.3 = (bf16[512,128]{1,0:T(8,128)(2,1)S(1)}, bf16[512,128]{1,0:T(8,128)(2,1)}, u32[]{:S(2)}) copy-start(bf16[512,128]{1,0:T(8,128)(2,1)} %w_out.5) | copy-start | bytes 393220
  0.7 11.0 %copy-start.4 = (s32[8,128]{1,0:T(8,128)S(1)}, s32[8,128]{1,0:T(8,128)}, u32[]{:S(2)}) copy-start(s32[8,128]{1,0:T(8,128)} %land.7) | copy-start | bytes 12292
  3.4 8.2 %copy-start.2 = (bf16[2,8,128,128]{3,2,1,0:T(8,128)(2,1)S(1)}, bf16[2,8,128,128]{3,2,1,0:T(8,128)(2,1)}, u32[]{:S(2)}) copy-start(bf16[2,8,128,128]{3,2,1,0:T(8,128)(2,1)} %get-tuple-element.35.rounded) | copy-start | bytes 1572868
  3.4 4.3 %collective-permute-start = (bf16[2,3,128,128]{3,2,1,0:T(8,128)(2,1)}, bf16[2,3,128,128]{3,2,1,0:T(8,128)(2,1)S(1)}, u32[]{:S(2)}, u32[]{:S(2)}) collective-permute-start(bf16[2,3,128,128]{3,2,1,0:T(8,128)(2,1)} %get-tuple-element.36), channel_id=1, source_target_pairs={{0,1},{1,2},{2,3},{3,4},{4,5},{5,6},{6,7},{7,8},{8,9},{9,10},{10,1... | collective-permute-start | bytes 589832 | tf_op jit(solution)/shard_map/ppermute | solution.py:426
  6.0 5.7 %collective-permute-start.1 = (bf16[2,3,128,128]{3,2,1,0:T(8,128)(2,1)}, bf16[2,3,128,128]{3,2,1,0:T(8,128)(2,1)S(1)}, u32[]{:S(2)}, u32[]{:S(2)}) collective-permute-start(bf16[2,3,128,128]{3,2,1,0:T(8,128)(2,1)} %get-tuple-element.37), channel_id=1, source_target_pairs={{1,0},{2,1},{3,2},{4,3},{5,4},{6,5},{7,6},{8,7},{9,8},{10,9},{11,1... | collective-permute-start | bytes 589832 | tf_op jit(solution)/shard_map/ppermute | solution.py:427
  18.2 9.3 %collective-permute-start.3 = (bf16[8,128,128]{2,1,0:T(8,128)(2,1)}, bf16[8,128,128]{2,1,0:T(8,128)(2,1)S(1)}, u32[]{:S(2)}, u32[]{:S(2)}) collective-permute-start(bf16[8,128,128]{2,1,0:T(8,128)(2,1)} %get-tuple-element.41), channel_id=1, source_target_pairs={{16,0},{17,1},{18,2},{19,3},{20,4},{21,5},{22,6},{23,7},{24,8},{25... | collective-permute-start | bytes 786440 | tf_op jit(solution)/shard_map/ppermute | solution.py:436
  26.1 8.6 %collective-permute-start.2 = (bf16[8,128,128]{2,1,0:T(8,128)(2,1)}, bf16[8,128,128]{2,1,0:T(8,128)(2,1)}, u32[]{:S(2)}, u32[]{:S(2)}) collective-permute-start(bf16[8,128,128]{2,1,0:T(8,128)(2,1)} %get-tuple-element.40), channel_id=1, source_target_pairs={{16,0},{17,1},{18,2},{19,3},{20,4},{21,5},{22,6},{23,7},{24,8},{25... | collective-permute-start | bytes 786440 | tf_op jit(solution)/shard_map/ppermute | solution.py:436
  43.8 4.8 %collective-permute-start.4 = (bf16[8,88,512]{2,1,0:T(8,128)(2,1)S(1)}, bf16[8,88,512]{2,1,0:T(8,128)(2,1)S(1)}, u32[]{:S(2)}, u32[]{:S(2)}) collective-permute-start(bf16[8,88,512]{2,1,0:T(8,128)(2,1)S(1)} %get-tuple-element.47), channel_id=1, source_target_pairs={{0,1},{1,0},{2,3},{3,2},{4,5},{5,4},{6,7},{7,6},{8,9},{9,8},{10,11... | collective-permute-start | bytes 2162696 | tf_op jit(solution)/shard_map/ppermute | solution.py:445
  49.0 10.0 %collective-permute-start.5 = (bf16[4,88,512]{2,1,0:T(8,128)(2,1)S(1)}, bf16[4,88,512]{2,1,0:T(8,128)(2,1)S(1)}, u32[]{:S(2)}, u32[]{:S(2)}) collective-permute-start(bf16[4,88,512]{2,1,0:T(8,128)(2,1)S(1)} %slice.39), channel_id=1, source_target_pairs={{0,2},{1,5},{2,0},{3,7},{4,6},{5,1},{6,4},{7,3},{8,10},{9,13},{10,... | collective-permute-start | bytes 1081352 | tf_op jit(solution)/shard_map/ppermute | solution.py:445
  52.6 4.4 %collective-permute-start.6 = (bf16[2,128,128]{2,1,0:T(8,128)(2,1)S(1)}, bf16[2,128,128]{2,1,0:T(8,128)(2,1)S(1)}, u32[]{:S(2)}, u32[]{:S(2)}) collective-permute-start(bf16[2,128,128]{2,1,0:T(8,128)(2,1)S(1)} %get-tuple-element.51), channel_id=1, source_target_pairs={{0,1},{1,2},{2,3},{3,4},{4,5},{5,6},{6,7},{7,8},{8,9},{9,10},{10,1... | collective-permute-start | bytes 196616 | tf_op jit(solution)/shard_map/ppermute | solution.py:454
  55.8 3.1 %collective-permute-start.7 = (bf16[2,128,128]{2,1,0:T(8,128)(2,1)S(1)}, bf16[2,128,128]{2,1,0:T(8,128)(2,1)S(1)}, u32[]{:S(2)}, u32[]{:S(2)}) collective-permute-start(bf16[2,128,128]{2,1,0:T(8,128)(2,1)S(1)} %get-tuple-element.52), channel_id=1, source_target_pairs={{1,0},{2,1},{3,2},{4,3},{5,4},{6,5},{7,6},{8,7},{9,8},{10,9},{11,1... | collective-permute-start | bytes 196616 | tf_op jit(solution)/shard_map/ppermute | solution.py:455
  59.1 8.4 %collective-permute-start.8 = (bf16[2,88,512]{2,1,0:T(8,128)(2,1)S(1)}, bf16[2,88,512]{2,1,0:T(8,128)(2,1)S(1)}, u32[]{:S(2)}, u32[]{:S(2)}) collective-permute-start(bf16[2,88,512]{2,1,0:T(8,128)(2,1)S(1)} %slice.40), channel_id=1, source_target_pairs={{0,4},{1,3},{2,6},{3,1},{4,0},{5,7},{6,2},{7,5},{8,12},{9,11},{10,... | collective-permute-start | bytes 540680 | tf_op jit(solution)/shard_map/ppermute | solution.py:445
  67.6 8.1 %collective-permute-start.9 = (bf16[1,88,512]{2,1,0:T(8,128)(2,1)S(1)}, bf16[1,88,512]{2,1,0:T(8,128)(2,1)S(1)}, u32[]{:S(2)}, u32[]{:S(2)}) collective-permute-start(bf16[1,88,512]{2,1,0:T(8,128)(2,1)S(1)} %slice.41), channel_id=1, source_target_pairs={{0,8},{1,9},{2,10},{3,11},{4,12},{5,13},{6,14},{7,15},{8,0},{9,1},... | collective-permute-start | bytes 270344 | tf_op jit(solution)/shard_map/ppermute | solution.py:445
  75.6 4.7 %collective-permute-start.10 = (bf16[1,88,512]{2,1,0:T(8,128)(2,1)S(1)}, bf16[1,88,512]{2,1,0:T(8,128)(2,1)S(1)}, u32[]{:S(2)}, u32[]{:S(2)}) collective-permute-start(bf16[1,88,512]{2,1,0:T(8,128)(2,1)S(1)} %get-tuple-element.66), channel_id=1, source_target_pairs={{0,16},{16,0},{1,17},{17,1},{2,18},{18,2},{3,19},{19,3},{4,20},{20... | collective-permute-start | bytes 270344 | tf_op jit(solution)/shard_map/ppermute | solution.py:466
where the time goes:
time: 81.4 us; the launch traced here: 81.1 us
  Pallas kernels  30.8 us (38%)
  waiting for transfers between devices  24.9 us (31%)
  starting transfers between devices  24 us (29%)
  between operations  0.88 us (1%)
    pallas_call x2, Pallas kernels, forward(): pl.pallas_call(forward_body, grid=(1,), in_specs=specs, out_specs=[full_b...  13.1 us
    ppermute x4, starting transfers between devices, exchanged(): lax.ppermute(value, 'tile', [(t, t ^ 1 << bits[t & 1]) for t in range(til...  12.9 us
    pallas_call x1, Pallas kernels, weight(): pl.pallas_call(functools.partial(weight_body, members, parts), grid_spec=...  9.18 us
    ppermute x4, waiting for transfers between devices, exchanged(): lax.ppermute(value, 'tile', [(t, t ^ 1 << bits[t & 1]) for t in range(til...  7.42 us
    ppermute x2, waiting for transfers between devices, shards(): mains.append(lax.ppermute(main, 'lead', steps))  7.1 us
    pallas_call x1, Pallas kernels, state_grad(): pl.pallas_call(functools.partial(state_body, len(pres)), grid=(1,), in_sp...  4.7 us
    ppermute x1, waiting for transfers between devices, shards(): lax.ppermute(total.astype(BF16), 'lead', [(s, leads - 1 - s) for s in ran...  4.66 us
    ppermute x1, waiting for transfers between devices, shards(): high = lax.ppermute(top, 'tile', behind)  3.88 us
  transfers between devices with their start and end apart: 11, of which 6 were waited for; matrix products, arithmetic and copies ran while one was open for 0% of the time, Pallas kernels for 14%

commit v1 on v0

--- a/solution.py
+++ b/solution.py
@@ -8,10 +8,12 @@
 from jax.experimental.pallas import tpu as pltpu
 from jax.sharding import PartitionSpec as P
 
+
 TANH_SCALE = 0.7978845608028654
 CUBIC_TERM = 0.044715
 BF16 = jnp.bfloat16
 F32 = jnp.float32
+STATE_STEP = 3
 PARAMS = pltpu.CompilerParams(vmem_limit_bytes=32 * 1024 * 1024)
 
 
@@ -25,15 +27,10 @@
 
 def gelu_pair(v):
     square = v * v
-    t = jnp.tanh(TANH_SCALE * (v + CUBIC_TERM * (square * v)))
-    half = 0.5 * (1.0 + t)
-    slope = half + (0.5 * v) * (1.0 - t * t) * (TANH_SCALE * (1.0 + 3.0 * CUBIC_TERM * square))
-    return v * half, slope
-
-
-def member_block(shape, member):
-    rest = len(shape) - 1
-    return pl.BlockSpec((1,) + tuple(shape[1:]), lambda i: (member,) + (0,) * rest)
+    half = 0.5 + 0.5 * jnp.tanh(v * (TANH_SCALE + (TANH_SCALE * CUBIC_TERM) * square))
+    value = v * half
+    slope = half + value * (1.0 - half) * (2.0 * TANH_SCALE + (6.0 * TANH_SCALE * CUBIC_TERM) * square)
+    return value, slope
 
 
 def full_block(shape):
@@ -54,8 +51,8 @@
             top[0, r] = value
         if r >= rows - 2:
             bottom[0, r - (rows - 2)] = value
-    top[0, 2] = masked_row(0, channels, cot, land, total_row(0, rows, channels, cot, 0))
-    bottom[0, 2] = masked_row(rows - 1, channels, cot, land, total_row(rows - 1, rows, channels, cot, 0))
+    top[0, 2] = masked_row(0, land, total_row(0, rows, channels, cot, 0))
+    bottom[0, 2] = masked_row(rows - 1, land, total_row(rows - 1, rows, channels, cot, 0))
 
 
 def prep(dates, section, forcing, states, cot, land):
@@ -139,7 +136,7 @@
     return total if main is None else total + main[r].astype(F32)
 
 
-def masked_row(r, channels, cot, land, total):
+def masked_row(r, land, total):
     return (land[r : r + 1, :].astype(F32) * total).astype(BF16)
 
 
@@ -160,17 +157,17 @@
 
 
 def forward_body(
-    rounded, low, high, turned, column, w_conv, w_out, cot, land,
+    member, rounded, low, high, turned, column, w_conv, w_out, cot, land,
     main, hidden_out, slope_out, stack, hidden, slope, masked, pre, z, sems,
 ):
     _, rows, channels, lon = rounded.shape
-    build_stack(rounded, low, high, stack, 0, 2)
-    masked[:, 0:lon] = low[0, 2]
+    build_stack(rounded, low, high, stack, member, 2)
+    masked[:, 0:lon] = low[member, 2]
     for r in range(rows):
         masked[:, (r + 1) * lon : (r + 2) * lon] = masked_row(
-            r, channels, cot, land, total_row(r, rows, channels, cot, 0)
+            r, land, total_row(r, rows, channels, cot, member)
         )
-    masked[:, (rows + 1) * lon :] = high[0, 2]
+    masked[:, (rows + 1) * lon :] = high[member, 2]
     bias = jnp.concatenate([column[...], column[...]], axis=1)
     for k in range(0, rows + 2, 2):
         preact = bias
@@ -192,7 +189,7 @@
     for copy in copies:
         copy.start()
     for r, grad in enumerate(own_grads(w_conv, pre, z, channels, rows, lon, 1)):
-        main[r] = (grad + total_row(r, rows, channels, cot, 0)).astype(BF16)
+        main[r] = (grad + total_row(r, rows, channels, cot, member)).astype(BF16)
     for copy in copies:
         copy.wait()
 
@@ -202,13 +199,11 @@
     taps, width = w_conv.shape
     cols, more = rows * lon, (rows + 2) * lon
     operands = [rounded, low, high, turned, column, w_conv, w_out, cot, land]
-    specs = [member_block(x.shape, member) for x in (rounded, low, high)]
-    specs += [full_block(x.shape) for x in (turned, column, w_conv, w_out)]
-    specs += [member_block(cot.shape, member), full_block(land.shape)]
+    specs = [full_block(x.shape) for x in operands]
     main = (rows, channels, lon)
     hbm = pl.BlockSpec(memory_space=pltpu.HBM)
     return pl.pallas_call(
-        forward_body,
+        functools.partial(forward_body, member),
         grid=(1,),
         in_specs=specs,
         out_specs=[full_block(main), hbm, hbm],
@@ -223,7 +218,6 @@
             pltpu.SemaphoreType.DMA((2,)),
         ],
         compiler_params=PARAMS,
-        name=f"forward_{member}",
     )(*operands)
 
 
@@ -246,44 +240,55 @@
     return place
 
 
-def weight_body(members, parts, here_ref, rounded, low, high, cot, land, w_out, w_conv, *refs):
-    mains, held = refs[:members], refs[members : 3 * members]
-    give, keep, up, down = refs[3 * members : 3 * members + 4]
-    pres = refs[3 * members + 4 : 4 * members + 4]
-    refs = refs[4 * members + 4 :]
-    local = refs[: 2 * members]
-    stack, masked, w1, w2, sems = refs[2 * members :]
+def weight_body(member, first, last, parts, here_ref, *refs):
+    rounded, low, high, cot, land, w_out, w_conv, main, hidden_in, slope_in = refs[:10]
+    refs = refs[10:]
+    if not first:
+        up_in, down_in, w1_in, w2_in, acc_in = refs[:5]
+        refs = refs[5:]
+        for m in range(member):
+            refs[0][m] = up_in[m]
+            refs[1][m] = down_in[m]
+    up, down, pre = refs[:3]
+    if last:
+        give, keep, hidden, slope, stack, masked, sems, w1, w2 = refs[3:]
+    else:
+        w1, w2, acc_out, hidden, slope, stack, masked, sems = refs[3:]
     _, rows, channels, lon = rounded.shape
     width = w_out.shape[0]
     cols = rows * lon
-    copies = [pltpu.make_async_copy(a, b, sems.at[i]) for i, (a, b) in enumerate(zip(held, local))]
+    copies = [
+        pltpu.make_async_copy(hidden_in, hidden, sems.at[0]),
+        pltpu.make_async_copy(slope_in, slope, sems.at[1]),
+    ]
     for copy in copies:
         copy.start()
-    acc = None
-    for m in range(members):
-        hidden, slope = local[2 * m : 2 * m + 2]
-        build_stack(rounded, low, high, stack.at[m], m, 1)
-        for r in range(rows):
-            masked[m, :, r * lon : (r + 1) * lon] = masked_row(
-                r, channels, cot, land, total_row(r, rows, channels, cot, m, mains[m])
-            )
-        copies[2 * m].wait()
-        part = dot_t(hidden[...], masked[m])
-        w2[...] = part if m == 0 else part + w2[...]
-        copies[2 * m + 1].wait()
-        for k in range(0, rows, 2):
-            at = slice(k * lon, (k + 2) * lon)
-            grad = dot(w_out[...], masked[m, :, at]) * slope[:, at]
-            pres[m][:, at] = grad.astype(BF16)
-            both = grad[:, :lon] + grad[:, lon:]
-            acc = both if acc is None else acc + both
-        above, below = edge_grads(w_conv, pres[m], channels, rows, lon)
-        up[m] = above.astype(BF16)
-        down[m] = below.astype(BF16)
-        for rs in range(3):
-            at = slice(rs * 3 * channels, (rs + 1) * 3 * channels)
-            part = dot_t(stack[m, :, rs * lon : rs * lon + cols], pres[m][...])
-            w1[at, :] = part if m == 0 else part + w1[at, :]
+    build_stack(rounded, low, high, stack, member, 1)
+    for r in range(rows):
+        masked[:, r * lon : (r + 1) * lon] = masked_row(
+            r, land, total_row(r, rows, channels, cot, member, main)
+        )
+    copies[0].wait()
+    part = dot_t(hidden[...], masked[...])
+    w2[...] = part if first else part + w2_in[...]
+    acc = None if first else acc_in[...]
+    copies[1].wait()
+    for k in range(0, rows, 2):
+        at = slice(k * lon, (k + 2) * lon)
+        grad = dot(w_out[...], masked[:, at]) * slope[:, at]
+        pre[:, at] = grad.astype(BF16)
+        both = grad[:, :lon] + grad[:, lon:]
+        acc = both if acc is None else acc + both
+    above, below = edge_grads(w_conv, pre, channels, rows, lon)
+    up[member] = above.astype(BF16)
+    down[member] = below.astype(BF16)
+    for rs in range(3):
+        at = slice(rs * 3 * channels, (rs + 1) * 3 * channels)
+        part = dot_t(stack[:, rs * lon : rs * lon + cols], pre[...])
+        w1[at, :] = part if first else part + w1_in[at, :]
+    if not last:
+        acc_out[...] = acc
+        return
 
     here = here_ref[0]
     core = here & 1
@@ -319,48 +324,54 @@
     return -(-used // 8) * 8
 
 
-def weight(here, parts, rounded, low, high, cot, land, w_out, w_conv, mains, kept):
+def weight(member, here, parts, rounded, low, high, cot, land, w_out, w_conv, main, kept, before):
     members, rows, channels, lon = rounded.shape
     taps, width = w_conv.shape
     cols = rows * lon
+    first, last = member == 0, member + 1 == members
 
     def full(shape):
         return pl.BlockSpec(tuple(shape), lambda i, _: (0,) * len(shape))
 
-    operands = [rounded, low, high, cot, land, w_out, w_conv, *mains]
+    operands = [rounded, low, high, cot, land, w_out, w_conv, main]
     specs = [full(x.shape) for x in operands]
-    held = [x for row in kept for x in row]
-    operands += [pltpu.with_memory_space_constraint(x, pltpu.HBM) for x in held]
-    specs += [pl.BlockSpec(memory_space=pltpu.HBM) for _ in held]
-    chunk = (parts // 2, packed_rows(taps, width, channels, parts), width)
-    edge = (members, channels, lon)
-    shapes = [(chunk, BF16), (chunk, F32), (edge, BF16), (edge, BF16)] + [((width, cols), BF16)] * members
+    operands += [pltpu.with_memory_space_constraint(x, pltpu.HBM) for x in kept]
+    specs += [pl.BlockSpec(memory_space=pltpu.HBM) for _ in kept]
+    operands += before
+    specs += [full(x.shape) for x in before]
+    edge = (member + 1, channels, lon)
+    sums = [((taps, width), F32), ((width, channels), F32)]
+    shapes = [(edge, BF16), (edge, BF16), ((width, cols), BF16)]
+    if last:
+        chunk = (parts // 2, packed_rows(taps, width, channels, parts), width)
+        shapes += [(chunk, BF16), (chunk, F32)]
+    else:
+        shapes += sums + [((width, lon), F32)]
     return pl.pallas_call(
-        functools.partial(weight_body, members, parts),
+        functools.partial(weight_body, member, first, last, parts),
         grid_spec=pltpu.PrefetchScalarGridSpec(
             num_scalar_prefetch=1,
             grid=(1,),
             in_specs=specs,
             out_specs=[full(s) for s, _ in shapes],
-            scratch_shapes=[pltpu.VMEM(x.shape, x.dtype) for x in held]
+            scratch_shapes=[pltpu.VMEM(x.shape, x.dtype) for x in kept]
             + [
-                pltpu.VMEM((members, 3 * channels, (rows + 2) * lon), BF16),
-                pltpu.VMEM((members, channels, cols), BF16),
-                pltpu.VMEM((taps, width), F32),
-                pltpu.VMEM((width, channels), F32),
-                pltpu.SemaphoreType.DMA((len(held),)),
-            ],
+                pltpu.VMEM((3 * channels, (rows + 2) * lon), BF16),
+                pltpu.VMEM((channels, cols), BF16),
+                pltpu.SemaphoreType.DMA((2,)),
+            ]
+            + ([pltpu.VMEM(s, d) for s, d in sums] if last else []),
         ),
         out_shape=[jax.ShapeDtypeStruct(s, d) for s, d in shapes],
         compiler_params=PARAMS,
-        name="weight",
     )(here, *operands)
 
 
 def state_body(members, w_conv, cot, beside_low, beside_high, *refs):
     pres, mains = refs[:members], refs[members : 2 * members]
-    out, z = refs[2 * members :]
+    out, z, local, sems = refs[2 * members :]
     rows, channels, lon = mains[0].shape
+    copies = [pltpu.make_async_copy(local.at[m], out.at[m], sems.at[m]) for m in range(members)]
     for m in range(members):
         for r, grad in enumerate(own_grads(w_conv, pres[m], z.at[m % 2], channels, rows, lon, 0)):
             total = grad + total_row(r, rows, channels, cot, m, mains[m])
@@ -368,7 +379,10 @@
                 total = total + beside_low[m].astype(F32)
             if r == rows - 1:
                 total = total + beside_high[m].astype(F32)
-            out[m, pl.ds(r, channels, stride=rows), :] = total
+            local[m, pl.ds(r, channels, stride=rows), :] = total
+        copies[m].start()
+    for copy in copies:
+        copy.wait()
 
 
 def state_grad(w_conv, cot, beside_low, beside_high, pres, mains):
@@ -378,9 +392,13 @@
         functools.partial(state_body, len(pres)),
         grid=(1,),
         in_specs=[full_block(x.shape) for x in operands],
-        out_specs=full_block(cot.shape),
-        out_shape=jax.ShapeDtypeStruct(cot.shape, F32),
-        scratch_shapes=[pltpu.VMEM((2, taps, pres[0].shape[1]), F32)],
+        out_specs=pl.BlockSpec(memory_space=pltpu.HBM),
+        out_shape=pltpu.HBM(cot.shape, F32),
+        scratch_shapes=[
+            pltpu.VMEM((2, taps, pres[0].shape[1]), F32),
+            pltpu.VMEM(cot.shape, F32),
+            pltpu.SemaphoreType.DMA((len(pres),)),
+        ],
         compiler_params=PARAMS,
         name="state",
     )(*operands)
@@ -434,32 +452,34 @@
         main, hidden, slope = forward(m, rounded, low, high, turned, column, w_conv, w_out, cot, land)
         kept.append((hidden, slope))
         mains.append(lax.ppermute(main, "lead", steps))
-    give, keep, up, down, *pres = weight(
-        here[None], tiles, rounded, low, high, cot, land, w_out, w_conv, mains, kept
-    )
-
+    before = []
+    pres = []
+    for m in range(members):
+        up, down, pre, *sums = weight(
+            m, here[None], tiles, rounded, low, high, cot, land, w_out, w_conv, mains[m], kept[m], before
+        )
+        before = [up, down, *sums]
+        pres.append(pre)
+    give, keep = sums
     assert tiles >= 8
 
     def exchanged(value, step):
         bits = (phase_bits(tiles, 0)[step], phase_bits(tiles, 1)[step])
         return lax.ppermute(value, "tile", [(t, t ^ (1 << bits[t & 1])) for t in range(tiles)])
 
-    depth = tiles.bit_length() - 1
     total = keep + exchanged(give, 0).astype(F32)
-    for step in range(1, depth):
+    for step in range(1, tiles.bit_length() - 1):
         half = total.shape[0] // 2
         send = total[half:].astype(BF16)
         if step == 1:
             send, up, down = lax.optimization_barrier((send, up, down))
             beside_low = lax.ppermute(down, "tile", ahead)
             beside_high = lax.ppermute(up, "tile", behind)
-        if step == 2:
-            send, beside_low, beside_high = lax.optimization_barrier((send, beside_low, beside_high))
+        if step == STATE_STEP:
+            send, *pres = lax.optimization_barrier((send, *pres))
             body = state_grad(w_conv, cot, beside_low, beside_high, pres, mains)
         taken = exchanged(send, step)
-        if step == 1:
-            taken, beside_low, beside_high = lax.optimization_barrier((taken, beside_low, beside_high))
-        if step == 2:
+        if step == STATE_STEP:
             taken, body = lax.optimization_barrier((taken, body))
         total = total[:half] + taken.astype(F32)
     grads = body.reshape(states.shape)

time: 81.4 us -> 82.7 us (1.016)
  the two profiles are of different devices: /device:TPU:0 before, /device:TPU:5 now
where the time goes in v1:
time: 82.7 us; the launch traced here: 82.4 us
  Pallas kernels  31.5 us (38%)
  waiting for transfers between devices  27.8 us (34%)
  starting transfers between devices  21.7 us (26%)
  between operations  0.9 us (1%)
    pallas_call x2, Pallas kernels, forward(): pl.pallas_call(functools.partial(forward_body, member), grid=(1,), in_spe...  12.6 us
    ppermute x4, waiting for transfers between devices, exchanged(): lax.ppermute(value, 'tile', [(t, t ^ 1 << bits[t & 1]) for t in range(til...  11.3 us
    pallas_call x2, Pallas kernels, weight(): pl.pallas_call(functools.partial(weight_body, member, first, last, parts)...  10.5 us
    ppermute x1, starting transfers between devices, shards(): beside_low = lax.ppermute(down, 'tile', ahead)  6.47 us
    ppermute x1, waiting for transfers between devices, shards(): high = lax.ppermute(top, 'tile', behind)  5.19 us
    ppermute x4, starting transfers between devices, exchanged(): lax.ppermute(value, 'tile', [(t, t ^ 1 << bits[t & 1]) for t in range(til...  4.71 us
    ppermute x1, waiting for transfers between devices, shards(): beside_high = lax.ppermute(up, 'tile', behind)  4.54 us
    pallas_call x1, Pallas kernels, state_grad(): pl.pallas_call(functools.partial(state_body, len(pres)), grid=(1,), in_sp...  4.52 us
  transfers between devices with their start and end apart: 11, of which 8 were waited for; matrix products, arithmetic and copies ran while one was open for 0% of the time, Pallas kernels for 19%

profile of v1, /device:TPU:5, one launch (start us, length us, event | category | flops | bytes accessed | tf_op | source)
XLA Modules:
  0.0 82.4 jit_solution(4066621783414832942)
XLA Ops:
  0.7 2.8 %prep.1 = (bf16[2,8,128,128]{3,2,1,0:T(8,128)(2,1)}, bf16[2,3,128,128]{3,2,1,0:T(8,128)(2,1)}, bf16[2,3,128,128]{3,2,1,0:T(8,128)(2,1)}) custom-call(s32[2]{0:T(128)} %dates.1, s32[1]{0:T(128)} %bitcast.1.section, f32[365,128]{1,0:T(8,128)} %forcing.1, f32[2,1024,128]{2,1,0:T(8,128)} %bitcast.14, f32[2,1024,128]{2,1,0:T(8,128)} %bitcast.7, s32[8,128]{1,0:T(8,128)} %refs_4_.3), custom_call_target="tpu_custom_call" | custom-call | tf_op jit(solution)/shard_map/prep/pallas_call | solution.py:65
  3.4 3.8 %collective-permute-start = (bf16[2,3,128,128]{3,2,1,0:T(8,128)(2,1)}, bf16[2,3,128,128]{3,2,1,0:T(8,128)(2,1)S(1)}, u32[]{:S(2)}, u32[]{:S(2)}) collective-permute-start(bf16[2,3,128,128]{3,2,1,0:T(8,128)(2,1)} %get-tuple-element.38), channel_id=1, source_target_pairs={{0,1},{1,2},{2,3},{3,4},{4,5},{5,6},{6,7},{7,8},{8,9},{9,10},{10,1... | collective-permute-start | bytes 589832 | tf_op jit(solution)/shard_map/ppermute | solution.py:444
  7.3 1.9 %collective-permute-start.1 = (bf16[2,3,128,128]{3,2,1,0:T(8,128)(2,1)}, bf16[2,3,128,128]{3,2,1,0:T(8,128)(2,1)S(1)}, u32[]{:S(2)}, u32[]{:S(2)}) collective-permute-start(bf16[2,3,128,128]{3,2,1,0:T(8,128)(2,1)} %get-tuple-element.39), channel_id=1, source_target_pairs={{1,0},{2,1},{3,2},{4,3},{5,4},{6,5},{7,6},{8,7},{9,8},{10,9},{11,1... | collective-permute-start | bytes 589832 | tf_op jit(solution)/shard_map/ppermute | solution.py:445
  9.2 0.4 turn.1
  9.7 0.5 collective-permute-done.low.refs_1_
  10.2 5.2 %collective-permute-done.1.high.refs_2_ = bf16[2,3,128,128]{3,2,1,0:T(8,128)(2,1)S(1)} collective-permute-done((bf16[2,3,128,128]{3,2,1,0:T(8,128)(2,1)}, bf16[2,3,128,128]{3,2,1,0:T(8,128)(2,1)S(1)}, u32[]{:S(2)}, u32[]{:S(2)}) %collective-permute-start.1) | collective-permute-done | bytes 196640 | tf_op jit(solution)/shard_map/ppermute | solution.py:445
  15.4 6.3 %shard_map.112 = (bf16[8,128,128]{2,1,0:T(8,128)(2,1)}, bf16[512,1024]{1,0:T(8,128)(2,1)}, f32[512,1024]{1,0:T(8,128)}) custom-call(bf16[2,8,128,128]{3,2,1,0:T(8,128)(2,1)S(1)} %copy-done.2, bf16[2,3,128,128]{3,2,1,0:T(8,128)(2,1)S(1)} %collective-permute-done.low.refs_1_, bf16[2,3,128,128]{3,2,1,0:T(8,128)(2,1)S(1)} %collective-permute-done.1.high.refs_2_, ...), custom_call_target="tpu_custom_call" | custom-call | tf_op jit(solution)/shard_map/pallas_call | solution.py:205
  21.7 1.3 %collective-permute-start.3 = (bf16[8,128,128]{2,1,0:T(8,128)(2,1)}, bf16[8,128,128]{2,1,0:T(8,128)(2,1)S(1)}, u32[]{:S(2)}, u32[]{:S(2)}) collective-permute-start(bf16[8,128,128]{2,1,0:T(8,128)(2,1)} %get-tuple-element.45), channel_id=1, source_target_pairs={{16,0},{17,1},{18,2},{19,3},{20,4},{21,5},{22,6},{23,7},{24,8},{25... | collective-permute-start | bytes 786440 | tf_op jit(solution)/shard_map/ppermute | solution.py:454
  23.0 6.3 %shard_map.111 = (bf16[8,128,128]{2,1,0:T(8,128)(2,1)}, bf16[512,1024]{1,0:T(8,128)(2,1)}, f32[512,1024]{1,0:T(8,128)}) custom-call(bf16[2,8,128,128]{3,2,1,0:T(8,128)(2,1)S(1)} %copy-done.2, bf16[2,3,128,128]{3,2,1,0:T(8,128)(2,1)S(1)} %collective-permute-done.low.refs_1_, bf16[2,3,128,128]{3,2,1,0:T(8,128)(2,1)S(1)} %collective-permute-done.1.high.refs_2_, ...), custom_call_target="tpu_custom_call" | custom-call | tf_op jit(solution)/shard_map/pallas_call | solution.py:205
  29.3 1.5 %collective-permute-start.2 = (bf16[8,128,128]{2,1,0:T(8,128)(2,1)}, bf16[8,128,128]{2,1,0:T(8,128)(2,1)}, u32[]{:S(2)}, u32[]{:S(2)}) collective-permute-start(bf16[8,128,128]{2,1,0:T(8,128)(2,1)} %get-tuple-element.42), channel_id=1, source_target_pairs={{16,0},{17,1},{18,2},{19,3},{20,4},{21,5},{22,6},{23,7},{24,8},{25... | collective-permute-start | bytes 786440 | tf_op jit(solution)/shard_map/ppermute | solution.py:454
  30.8 0.0 collective-permute-done.3.refs_7_.refs_2_
  30.8 4.2 %shard_map.113 = (bf16[1,128,128]{2,1,0:T(8,128)(2,1)S(1)}, bf16[1,128,128]{2,1,0:T(8,128)(2,1)S(1)}, bf16[512,1024]{1,0:T(8,128)(2,1)S(1)}, f32[1152,512]{1,0:T...) custom-call(s32[1]{0:T(128)} %bitcast.here_ref, bf16[2,8,128,128]{3,2,1,0:T(8,128)(2,1)S(1)} %copy-done.2, ...), custom_call_target="tpu_custom_call" | custom-call | tf_op jit(solution)/shard_map/pallas_call | solution.py:350
  35.0 3.0 %collective-permute-done.2.refs_7_.refs_3_ = bf16[8,128,128]{2,1,0:T(8,128)(2,1)} collective-permute-done((bf16[8,128,128]{2,1,0:T(8,128)(2,1)}, bf16[8,128,128]{2,1,0:T(8,128)(2,1)}, u32[]{:S(2)}, u32[]{:S(2)}) %collective-permute-start.2) | collective-permute-done | bytes 262176 | tf_op jit(solution)/shard_map/ppermute | solution.py:454
  38.0 6.3 %shard_map.114 = (bf16[2,128,128]{2,1,0:T(8,128)(2,1)S(1)}, bf16[2,128,128]{2,1,0:T(8,128)(2,1)S(1)}, bf16[512,1024]{1,0:T(8,128)(2,1)S(1)}, bf16[8,88,512]{2,1,0:T(8,128)(2,1)S(1)}, f32[8,88,512]{2,1,0:T(8,128)S(1)}) custom-call(s32[1]{0:T(128)} %bitcast.here_ref, bf16[2,8,128,128]{3,2,1,0:T(8,128)(2,1)S(1)} %copy-done.2, ...), custom_call_target="tpu_custom_call" | custom-call | tf_op jit(solution)/shard_map/pallas_call | solution.py:350
  44.3 0.1 collective-permute-start.4
  44.4 2.2 %collective-permute-done.4 = bf16[8,88,512]{2,1,0:T(8,128)(2,1)S(1)} collective-permute-done((bf16[8,88,512]{2,1,0:T(8,128)(2,1)S(1)}, bf16[8,88,512]{2,1,0:T(8,128)(2,1)S(1)}, u32[]{:S(2)}, u32[]{:S(2)}) %collective-permute-start.4) | collective-permute-done | bytes 720928 | tf_op jit(solution)/shard_map/ppermute | solution.py:468
  46.6 0.2 convert_add_fusion
  46.8 1.4 %collective-permute-start.5 = (bf16[4,88,512]{2,1,0:T(8,128)(2,1)S(1)}, bf16[4,88,512]{2,1,0:T(8,128)(2,1)S(1)}, u32[]{:S(2)}, u32[]{:S(2)}) collective-permute-start(bf16[4,88,512]{2,1,0:T(8,128)(2,1)S(1)} %slice.39), channel_id=1, source_target_pairs={{0,2},{1,5},{2,0},{3,7},{4,6},{5,1},{6,4},{7,3},{8,10},{9,13},{10,... | collective-permute-start | bytes 1081352 | tf_op jit(solution)/shard_map/ppermute | solution.py:468
  48.2 5.3 %collective-permute-done.5 = bf16[4,88,512]{2,1,0:T(8,128)(2,1)S(1)} collective-permute-done((bf16[4,88,512]{2,1,0:T(8,128)(2,1)S(1)}, bf16[4,88,512]{2,1,0:T(8,128)(2,1)S(1)}, u32[]{:S(2)}, u32[]{:S(2)}) %collective-permute-start.5) | collective-permute-done | bytes 360480 | tf_op jit(solution)/shard_map/ppermute | solution.py:468
  53.5 0.1 slice_add_fusion
  53.6 0.9 %collective-permute-start.6 = (bf16[2,88,512]{2,1,0:T(8,128)(2,1)S(1)}, bf16[2,88,512]{2,1,0:T(8,128)(2,1)S(1)}, u32[]{:S(2)}, u32[]{:S(2)}) collective-permute-start(bf16[2,88,512]{2,1,0:T(8,128)(2,1)S(1)} %slice.40), channel_id=1, source_target_pairs={{0,4},{1,3},{2,6},{3,1},{4,0},{5,7},{6,2},{7,5},{8,12},{9,11},{10,... | collective-permute-start | bytes 540680 | tf_op jit(solution)/shard_map/ppermute | solution.py:468
  54.5 3.8 %collective-permute-done.6 = bf16[2,88,512]{2,1,0:T(8,128)(2,1)S(1)} collective-permute-done((bf16[2,88,512]{2,1,0:T(8,128)(2,1)S(1)}, bf16[2,88,512]{2,1,0:T(8,128)(2,1)S(1)}, u32[]{:S(2)}, u32[]{:S(2)}) %collective-permute-start.6) | collective-permute-done | bytes 180256 | tf_op jit(solution)/shard_map/ppermute | solution.py:468
  58.4 2.4 %collective-permute-start.7 = (bf16[1,88,512]{2,1,0:T(8,128)(2,1)S(1)}, bf16[1,88,512]{2,1,0:T(8,128)(2,1)S(1)}, u32[]{:S(2)}, u32[]{:S(2)}) collective-permute-start(bf16[1,88,512]{2,1,0:T(8,128)(2,1)S(1)} %slice.41), channel_id=1, source_target_pairs={{0,8},{1,9},{2,10},{3,11},{4,12},{5,13},{6,14},{7,15},{8,0},{9,1},... | collective-permute-start | bytes 270344 | tf_op jit(solution)/shard_map/ppermute | solution.py:468
  60.8 6.5 %collective-permute-start.8 = (bf16[2,128,128]{2,1,0:T(8,128)(2,1)S(1)}, bf16[2,128,128]{2,1,0:T(8,128)(2,1)S(1)}, u32[]{:S(2)}, u32[]{:S(2)}) collective-permute-start(bf16[2,128,128]{2,1,0:T(8,128)(2,1)S(1)} %get-tuple-element.61), channel_id=1, source_target_pairs={{0,1},{1,2},{2,3},{3,4},{4,5},{5,6},{6,7},{7,8},{8,9},{9,10},{10,1... | collective-permute-start | bytes 196616 | tf_op jit(solution)/shard_map/ppermute | solution.py:476
  67.2 1.9 %collective-permute-start.9 = (bf16[2,128,128]{2,1,0:T(8,128)(2,1)S(1)}, bf16[2,128,128]{2,1,0:T(8,128)(2,1)S(1)}, u32[]{:S(2)}, u32[]{:S(2)}) collective-permute-start(bf16[2,128,128]{2,1,0:T(8,128)(2,1)S(1)} %get-tuple-element.62), channel_id=1, source_target_pairs={{1,0},{2,1},{3,2},{4,3},{5,4},{6,5},{7,6},{8,7},{9,8},{10,9},{11,1... | collective-permute-start | bytes 196616 | tf_op jit(solution)/shard_map/ppermute | solution.py:477
  69.2 0.0 collective-permute-done.8.beside_low
  69.2 4.5 %collective-permute-done.9.beside_high = bf16[2,128,128]{2,1,0:T(8,128)(2,1)S(1)} collective-permute-done((bf16[2,128,128]{2,1,0:T(8,128)(2,1)S(1)}, bf16[2,128,128]{2,1,0:T(8,128)(2,1)S(1)}, u32[]{:S(2)}, u32[]{:S(2)}) %collective-permute-start.9) | collective-permute-done | bytes 65568 | tf_op jit(solution)/shard_map/ppermute | solution.py:477
  73.7 4.5 %state.1 = f32[2,1024,128]{2,1,0:T(8,128)} custom-call(bf16[1152,512]{1,0:T(8,128)(2,1)S(1)} %copy-done, f32[2,1024,128]{2,1,0:T(8,128)S(1)} %bitcast.12, bf16[2,128,128]{2,1,0:T(8,128)(2,1)S(1)} %collective-permute-done.8.beside_low, bf16[2,128,128]{2,1,0:T(8,128)(2,1)S(1)} %collective-permute-done.9.beside_high, ...), custom_call_target="tpu_custom_call" | custom-call | tf_op jit(solution)/shard_map/state/pallas_call | solution.py:391
  78.2 0.0 collective-permute-done.7
  78.3 0.1 collective-permute-start.10
  78.4 3.4 %collective-permute-done.10.taken = bf16[1,88,512]{2,1,0:T(8,128)(2,1)S(1)} collective-permute-done((bf16[1,88,512]{2,1,0:T(8,128)(2,1)S(1)}, bf16[1,88,512]{2,1,0:T(8,128)(2,1)S(1)}, u32[]{:S(2)}, u32[]{:S(2)}) %collective-permute-start.10) | collective-permute-done | bytes 90144 | tf_op jit(solution)/shard_map/ppermute | solution.py:486
  81.7 0.7 finish.1
  (17 shorter events, 0.2 us)
Async XLA Ops:
  0.6 8.6 %copy-start = (bf16[1152,512]{1,0:T(8,128)(2,1)S(1)}, bf16[1152,512]{1,0:T(8,128)(2,1)}, u32[]{:S(2)}) copy-start(bf16[1152,512]{1,0:T(8,128)(2,1)} %w_conv.7) | copy-start | bytes 3538948
  0.6 8.6 %copy-start.5 = (f32[512]{0:T(512)S(1)}, f32[512]{0:T(512)}, u32[]{:S(2)}) copy-start(f32[512]{0:T(512)} %param.11) | copy-start | bytes 6148
  0.7 14.7 %copy-start.1 = (f32[1,2,128,8,128]{4,3,2,1,0:T(8,128)S(1)}, f32[1,2,128,8,128]{4,3,2,1,0:T(8,128)}, u32[]{:S(2)}) copy-start(f32[1,2,128,8,128]{4,3,2,1,0:T(8,128)} %param.9) | copy-start | bytes 3145732
  0.7 14.7 %copy-start.3 = (bf16[512,128]{1,0:T(8,128)(2,1)S(1)}, bf16[512,128]{1,0:T(8,128)(2,1)}, u32[]{:S(2)}) copy-start(bf16[512,128]{1,0:T(8,128)(2,1)} %refs_5_.3) | copy-start | bytes 393220
  0.7 14.7 %copy-start.4 = (s32[8,128]{1,0:T(8,128)S(1)}, s32[8,128]{1,0:T(8,128)}, u32[]{:S(2)}) copy-start(s32[8,128]{1,0:T(8,128)} %refs_4_.3) | copy-start | bytes 12292
  3.4 12.0 %copy-start.2 = (bf16[2,8,128,128]{3,2,1,0:T(8,128)(2,1)S(1)}, bf16[2,8,128,128]{3,2,1,0:T(8,128)(2,1)}, u32[]{:S(2)}) copy-start(bf16[2,8,128,128]{3,2,1,0:T(8,128)(2,1)} %get-tuple-element.37.rounded.refs_0_) | copy-start | bytes 1572868
  3.4 6.7 %collective-permute-start = (bf16[2,3,128,128]{3,2,1,0:T(8,128)(2,1)}, bf16[2,3,128,128]{3,2,1,0:T(8,128)(2,1)S(1)}, u32[]{:S(2)}, u32[]{:S(2)}) collective-permute-start(bf16[2,3,128,128]{3,2,1,0:T(8,128)(2,1)} %get-tuple-element.38), channel_id=1, source_target_pairs={{0,1},{1,2},{2,3},{3,4},{4,5},{5,6},{6,7},{7,8},{8,9},{9,10},{10,1... | collective-permute-start | bytes 589832 | tf_op jit(solution)/shard_map/ppermute | solution.py:444
  7.3 8.1 %collective-permute-start.1 = (bf16[2,3,128,128]{3,2,1,0:T(8,128)(2,1)}, bf16[2,3,128,128]{3,2,1,0:T(8,128)(2,1)S(1)}, u32[]{:S(2)}, u32[]{:S(2)}) collective-permute-start(bf16[2,3,128,128]{3,2,1,0:T(8,128)(2,1)} %get-tuple-element.39), channel_id=1, source_target_pairs={{1,0},{2,1},{3,2},{4,3},{5,4},{6,5},{7,6},{8,7},{9,8},{10,9},{11,1... | collective-permute-start | bytes 589832 | tf_op jit(solution)/shard_map/ppermute | solution.py:445
  21.7 9.1 %collective-permute-start.3 = (bf16[8,128,128]{2,1,0:T(8,128)(2,1)}, bf16[8,128,128]{2,1,0:T(8,128)(2,1)S(1)}, u32[]{:S(2)}, u32[]{:S(2)}) collective-permute-start(bf16[8,128,128]{2,1,0:T(8,128)(2,1)} %get-tuple-element.45), channel_id=1, source_target_pairs={{16,0},{17,1},{18,2},{19,3},{20,4},{21,5},{22,6},{23,7},{24,8},{25... | collective-permute-start | bytes 786440 | tf_op jit(solution)/shard_map/ppermute | solution.py:454
  29.3 8.6 %collective-permute-start.2 = (bf16[8,128,128]{2,1,0:T(8,128)(2,1)}, bf16[8,128,128]{2,1,0:T(8,128)(2,1)}, u32[]{:S(2)}, u32[]{:S(2)}) collective-permute-start(bf16[8,128,128]{2,1,0:T(8,128)(2,1)} %get-tuple-element.42), channel_id=1, source_target_pairs={{16,0},{17,1},{18,2},{19,3},{20,4},{21,5},{22,6},{23,7},{24,8},{25... | collective-permute-start | bytes 786440 | tf_op jit(solution)/shard_map/ppermute | solution.py:454
  44.3 2.3 %collective-permute-start.4 = (bf16[8,88,512]{2,1,0:T(8,128)(2,1)S(1)}, bf16[8,88,512]{2,1,0:T(8,128)(2,1)S(1)}, u32[]{:S(2)}, u32[]{:S(2)}) collective-permute-start(bf16[8,88,512]{2,1,0:T(8,128)(2,1)S(1)} %get-tuple-element.54), channel_id=1, source_target_pairs={{0,1},{1,0},{2,3},{3,2},{4,5},{5,4},{6,7},{7,6},{8,9},{9,8},{10,11... | collective-permute-start | bytes 2162696 | tf_op jit(solution)/shard_map/ppermute | solution.py:468
  46.8 6.6 %collective-permute-start.5 = (bf16[4,88,512]{2,1,0:T(8,128)(2,1)S(1)}, bf16[4,88,512]{2,1,0:T(8,128)(2,1)S(1)}, u32[]{:S(2)}, u32[]{:S(2)}) collective-permute-start(bf16[4,88,512]{2,1,0:T(8,128)(2,1)S(1)} %slice.39), channel_id=1, source_target_pairs={{0,2},{1,5},{2,0},{3,7},{4,6},{5,1},{6,4},{7,3},{8,10},{9,13},{10,... | collective-permute-start | bytes 1081352 | tf_op jit(solution)/shard_map/ppermute | solution.py:468
  53.6 4.7 %collective-permute-start.6 = (bf16[2,88,512]{2,1,0:T(8,128)(2,1)S(1)}, bf16[2,88,512]{2,1,0:T(8,128)(2,1)S(1)}, u32[]{:S(2)}, u32[]{:S(2)}) collective-permute-start(bf16[2,88,512]{2,1,0:T(8,128)(2,1)S(1)} %slice.40), channel_id=1, source_target_pairs={{0,4},{1,3},{2,6},{3,1},{4,0},{5,7},{6,2},{7,5},{8,12},{9,11},{10,... | collective-permute-start | bytes 540680 | tf_op jit(solution)/shard_map/ppermute | solution.py:468
  58.4 19.9 %collective-permute-start.7 = (bf16[1,88,512]{2,1,0:T(8,128)(2,1)S(1)}, bf16[1,88,512]{2,1,0:T(8,128)(2,1)S(1)}, u32[]{:S(2)}, u32[]{:S(2)}) collective-permute-start(bf16[1,88,512]{2,1,0:T(8,128)(2,1)S(1)} %slice.41), channel_id=1, source_target_pairs={{0,8},{1,9},{2,10},{3,11},{4,12},{5,13},{6,14},{7,15},{8,0},{9,1},... | collective-permute-start | bytes 270344 | tf_op jit(solution)/shard_map/ppermute | solution.py:468
  60.8 8.4 %collective-permute-start.8 = (bf16[2,128,128]{2,1,0:T(8,128)(2,1)S(1)}, bf16[2,128,128]{2,1,0:T(8,128)(2,1)S(1)}, u32[]{:S(2)}, u32[]{:S(2)}) collective-permute-start(bf16[2,128,128]{2,1,0:T(8,128)(2,1)S(1)} %get-tuple-element.61), channel_id=1, source_target_pairs={{0,1},{1,2},{2,3},{3,4},{4,5},{5,6},{6,7},{7,8},{8,9},{9,10},{10,1... | collective-permute-start | bytes 196616 | tf_op jit(solution)/shard_map/ppermute | solution.py:476
  67.2 6.5 %collective-permute-start.9 = (bf16[2,128,128]{2,1,0:T(8,128)(2,1)S(1)}, bf16[2,128,128]{2,1,0:T(8,128)(2,1)S(1)}, u32[]{:S(2)}, u32[]{:S(2)}) collective-permute-start(bf16[2,128,128]{2,1,0:T(8,128)(2,1)S(1)} %get-tuple-element.62), channel_id=1, source_target_pairs={{1,0},{2,1},{3,2},{4,3},{5,4},{6,5},{7,6},{8,7},{9,8},{10,9},{11,1... | collective-permute-start | bytes 196616 | tf_op jit(solution)/shard_map/ppermute | solution.py:477
  78.3 3.4 %collective-permute-start.10 = (bf16[1,88,512]{2,1,0:T(8,128)(2,1)S(1)}, bf16[1,88,512]{2,1,0:T(8,128)(2,1)S(1)}, u32[]{:S(2)}, u32[]{:S(2)}) collective-permute-start(bf16[1,88,512]{2,1,0:T(8,128)(2,1)S(1)} %get-tuple-element.70), channel_id=1, source_target_pairs={{0,16},{16,0},{1,17},{17,1},{2,18},{18,2},{3,19},{19,3},{4,20},{20... | collective-permute-start | bytes 270344 | tf_op jit(solution)/shard_map/ppermute | solution.py:486

commit v2 on v1

--- a/solution.py
+++ b/solution.py
@@ -107,24 +107,16 @@
     return out
 
 
-def own_grads(w_conv, pre, z, channels, rows, lon, halo):
-    taps = 9 * channels
-    for k in range(0, rows, 2):
-        cols = slice((k + halo) * lon, (k + halo + 2) * lon)
-        z[0:taps, cols] = dot(w_conv[...], pre[:, cols])
-    for source, rs in ((-1, 2), (rows, 0)) if halo else ():
-        cols = slice((source + 1) * lon, (source + 2) * lon)
-        block = slice(rs * 3 * channels, (rs + 1) * 3 * channels)
-        z[block, cols] = dot(w_conv[block, :], pre[:, cols])
+def row_sums(z, place, channels, rows, lon):
     for i in range(rows):
         per_step = []
         for cs in range(3):
             total = None
             for rs in range(3):
                 source = i - (rs - 1)
-                if -halo <= source < rows + halo:
+                if source in place:
                     tap = 3 * rs + cs
-                    at = (source + halo) * lon
+                    at = place[source] * lon
                     term = z[tap * channels : (tap + 1) * channels, at : at + lon]
                     total = term if total is None else total + term
             per_step.append(total)
@@ -140,81 +132,151 @@
     return (land[r : r + 1, :].astype(F32) * total).astype(BF16)
 
 
-def build_stack(rounded, low, high, stack, member, halo):
-    _, rows, channels, lon = rounded.shape
-    for q in range(-halo, rows + halo):
-        if q < 0:
-            x = low[member, 2 + q]
-        elif q >= rows:
-            x = high[member, q - rows]
-        else:
-            x = rounded[member, q]
+def state_line(q, rounded, low, high, member):
+    rows = rounded.shape[1]
+    if q < 0:
+        return low[member, 2 + q]
+    return high[member, q - rows] if q >= rows else rounded[member, q]
+
+
+def build_stack(lines, stack):
+    channels, lon = lines[0].shape
+    for q, x in enumerate(lines):
         wide = x.astype(F32)
-        at = slice((q + halo) * lon, (q + halo + 1) * lon)
+        at = slice(q * lon, (q + 1) * lon)
         stack[0:channels, at] = pltpu.roll(wide, 1, 1).astype(BF16)
         stack[channels : 2 * channels, at] = x
         stack[2 * channels : 3 * channels, at] = pltpu.roll(wide, lon - 1, 1).astype(BF16)
 
 
+def two_rows(turned, stack, start, bias, lon):
+    channels = stack.shape[0] // 3
+    preact = bias
+    for rs in range(3):
+        preact = preact + dot(
+            turned[:, rs * 3 * channels : (rs + 1) * 3 * channels],
+            stack[:, (start + rs) * lon : (start + rs + 2) * lon],
+        )
+    return gelu_pair(preact)
+
+
+def inner_body(members, rounded, turned, column, w_out, cot, land, *refs):
+    pres, hidden_out, slope_out = (refs[i * members : (i + 1) * members] for i in range(3))
+    stack, hidden, slope, masked, sems = refs[3 * members :]
+    _, rows, channels, lon = rounded.shape
+    bias = jnp.concatenate([column[...], column[...]], axis=1)
+    copies = []
+    for m in range(members):
+        build_stack([rounded[m, q] for q in range(rows)], stack.at[m])
+        for r in range(1, rows - 1):
+            masked[m, :, (r - 1) * lon : r * lon] = masked_row(
+                r, land, total_row(r, rows, channels, cot, m)
+            )
+        for k in range(0, rows - 2, 2):
+            value, steep = two_rows(turned, stack.at[m], k, bias, lon)
+            cols = slice(k * lon, (k + 2) * lon)
+            hidden[m, :, cols] = value.astype(BF16)
+            slope[m, :, cols] = steep
+            pres[m][:, cols] = (dot(w_out[...], masked[m, :, cols]) * steep).astype(BF16)
+        copies.append(pltpu.make_async_copy(hidden.at[m], hidden_out[m], sems.at[m, 0]))
+        copies.append(pltpu.make_async_copy(slope.at[m], slope_out[m], sems.at[m, 1]))
+        copies[-2].start()
+        copies[-1].start()
+    for copy in copies:
+        copy.wait()
+
+
+def inner(rounded, turned, column, w_out, cot, land):
+    members, rows, channels, lon = rounded.shape
+    assert rows % 2 == 0 and rows >= 4
+    width = turned.shape[0]
+    cols = (rows - 2) * lon
+    operands = [rounded, turned, column, w_out, cot, land]
+    hbm = pl.BlockSpec(memory_space=pltpu.HBM)
+    outs = pl.pallas_call(
+        functools.partial(inner_body, members),
+        grid=(1,),
+        in_specs=[full_block(x.shape) for x in operands],
+        out_specs=[full_block((width, cols))] * members + [hbm] * (2 * members),
+        out_shape=[jax.ShapeDtypeStruct((width, cols), BF16)] * members
+        + [pltpu.HBM((width, cols), BF16)] * members
+        + [pltpu.HBM((width, cols), F32)] * members,
+        scratch_shapes=[
+            pltpu.VMEM((members, 3 * channels, rows * lon), BF16),
+            pltpu.VMEM((members, width, cols), BF16),
+            pltpu.VMEM((members, width, cols), F32),
+            pltpu.VMEM((members, channels, cols), BF16),
+            pltpu.SemaphoreType.DMA((members, 2)),
+        ],
+        compiler_params=PARAMS,
+        name="inner",
+    )(*operands)
+    return outs[:members], outs[members : 2 * members], outs[2 * members :]
+
+
 def forward_body(
-    member, rounded, low, high, turned, column, w_conv, w_out, cot, land,
+    member, rounded, low, high, turned, column, w_conv, w_out, cot, land, pre_in,
     main, hidden_out, slope_out, stack, hidden, slope, masked, pre, z, sems,
 ):
     _, rows, channels, lon = rounded.shape
-    build_stack(rounded, low, high, stack, member, 2)
+    taps = 9 * channels
+    lines = [*range(-2, 2), *range(rows - 2, rows + 2)]
+    build_stack([state_line(q, rounded, low, high, member) for q in lines], stack)
     masked[:, 0:lon] = low[member, 2]
-    for r in range(rows):
-        masked[:, (r + 1) * lon : (r + 2) * lon] = masked_row(
+    for i, r in ((1, 0), (2, rows - 1)):
+        masked[:, i * lon : (i + 1) * lon] = masked_row(
             r, land, total_row(r, rows, channels, cot, member)
         )
-    masked[:, (rows + 1) * lon :] = high[member, 2]
+    masked[:, 3 * lon :] = high[member, 2]
     bias = jnp.concatenate([column[...], column[...]], axis=1)
-    for k in range(0, rows + 2, 2):
-        preact = bias
-        for rs in range(3):
-            preact = preact + dot(
-                turned[:, rs * 3 * channels : (rs + 1) * 3 * channels],
-                stack[:, (k + rs) * lon : (k + rs + 2) * lon],
-            )
-        value, steep = gelu_pair(preact)
-        cols = slice(k * lon, (k + 2) * lon)
+    for side in range(2):
+        value, steep = two_rows(turned, stack, 4 * side, bias, lon)
+        cols = slice(2 * side * lon, (2 * side + 2) * lon)
         hidden[:, cols] = value.astype(BF16)
         slope[:, cols] = steep
         pre[:, cols] = (dot(w_out[...], masked[:, cols]) * steep).astype(BF16)
-    inner = slice(lon, (rows + 1) * lon)
+    middle = slice(lon, 3 * lon)
     copies = [
-        pltpu.make_async_copy(hidden.at[:, inner], hidden_out, sems.at[0]),
-        pltpu.make_async_copy(slope.at[:, inner], slope_out, sems.at[1]),
+        pltpu.make_async_copy(hidden.at[:, middle], hidden_out, sems.at[0]),
+        pltpu.make_async_copy(slope.at[:, middle], slope_out, sems.at[1]),
     ]
     for copy in copies:
         copy.start()
-    for r, grad in enumerate(own_grads(w_conv, pre, z, channels, rows, lon, 1)):
+    place = {-1: 0, 0: 1, rows - 1: 2, rows: 3}
+    for k in range(0, rows - 2, 2):
+        place[k + 1], place[k + 2] = 4 + k, 5 + k
+        z[0:taps, (4 + k) * lon : (6 + k) * lon] = dot(w_conv[...], pre_in[:, k * lon : (k + 2) * lon])
+    z[0:taps, middle] = dot(w_conv[...], pre[:, middle])
+    for at, rs in ((0, 2), (3, 0)):
+        cols = slice(at * lon, (at + 1) * lon)
+        block = slice(rs * 3 * channels, (rs + 1) * 3 * channels)
+        z[block, cols] = dot(w_conv[block, :], pre[:, cols])
+    for r, grad in enumerate(row_sums(z, place, channels, rows, lon)):
         main[r] = (grad + total_row(r, rows, channels, cot, member)).astype(BF16)
     for copy in copies:
         copy.wait()
 
 
-def forward(member, rounded, low, high, turned, column, w_conv, w_out, cot, land):
+def forward(member, rounded, low, high, turned, column, w_conv, w_out, cot, land, pre_in):
     _, rows, channels, lon = rounded.shape
     taps, width = w_conv.shape
-    cols, more = rows * lon, (rows + 2) * lon
-    operands = [rounded, low, high, turned, column, w_conv, w_out, cot, land]
-    specs = [full_block(x.shape) for x in operands]
+    operands = [rounded, low, high, turned, column, w_conv, w_out, cot, land, pre_in]
     main = (rows, channels, lon)
     hbm = pl.BlockSpec(memory_space=pltpu.HBM)
+    kept = (width, 2 * lon)
     return pl.pallas_call(
         functools.partial(forward_body, member),
         grid=(1,),
-        in_specs=specs,
+        in_specs=[full_block(x.shape) for x in operands],
         out_specs=[full_block(main), hbm, hbm],
-        out_shape=[jax.ShapeDtypeStruct(main, BF16), pltpu.HBM((width, cols), BF16), pltpu.HBM((width, cols), F32)],
+        out_shape=[jax.ShapeDtypeStruct(main, BF16), pltpu.HBM(kept, BF16), pltpu.HBM(kept, F32)],
         scratch_shapes=[
-            pltpu.VMEM((3 * channels, (rows + 4) * lon), BF16),
-            pltpu.VMEM((width, more), BF16),
-            pltpu.VMEM((width, more), F32),
-            pltpu.VMEM((channels, more), BF16),
-            pltpu.VMEM((width, more), BF16),
-            pltpu.VMEM((taps, more), F32),
+            pltpu.VMEM((3 * channels, 8 * lon), BF16),
+            pltpu.VMEM((width, 4 * lon), BF16),
+            pltpu.VMEM((width, 4 * lon), F32),
+            pltpu.VMEM((channels, 4 * lon), BF16),
+            pltpu.VMEM((width, 4 * lon), BF16),
+            pltpu.VMEM((taps, (rows + 2) * lon), F32),
             pltpu.SemaphoreType.DMA((2,)),
         ],
         compiler_params=PARAMS,
@@ -241,8 +303,9 @@
 
 
 def weight_body(member, first, last, parts, here_ref, *refs):
-    rounded, low, high, cot, land, w_out, w_conv, main, hidden_in, slope_in = refs[:10]
-    refs = refs[10:]
+    rounded, low, high, cot, land, w_out, w_conv, main = refs[:8]
+    held = refs[8:12]
+    refs = refs[12:]
     if not first:
         up_in, down_in, w1_in, w2_in, acc_in = refs[:5]
         refs = refs[5:]
@@ -257,22 +320,31 @@
     _, rows, channels, lon = rounded.shape
     width = w_out.shape[0]
     cols = rows * lon
-    copies = [
-        pltpu.make_async_copy(hidden_in, hidden, sems.at[0]),
-        pltpu.make_async_copy(slope_in, slope, sems.at[1]),
-    ]
-    for copy in copies:
-        copy.start()
-    build_stack(rounded, low, high, stack, member, 1)
+    parts_of = [slice(lon, cols - lon), slice(0, lon), slice(cols - lon, cols)]
+    copies = []
+    for i, target in enumerate((hidden, slope)):
+        middle, outer = held[2 * i : 2 * i + 2]
+        sources = [middle, outer.at[:, 0:lon], outer.at[:, lon : 2 * lon]]
+        copies.append(
+            [
+                pltpu.make_async_copy(source, target.at[:, at], sems.at[i, j])
+                for j, (source, at) in enumerate(zip(sources, parts_of))
+            ]
+        )
+        for copy in copies[-1]:
+            copy.start()
+    build_stack([state_line(q, rounded, low, high, member) for q in range(-1, rows + 1)], stack)
     for r in range(rows):
         masked[:, r * lon : (r + 1) * lon] = masked_row(
             r, land, total_row(r, rows, channels, cot, member, main)
         )
-    copies[0].wait()
+    for copy in copies[0]:
+        copy.wait()
     part = dot_t(hidden[...], masked[...])
     w2[...] = part if first else part + w2_in[...]
     acc = None if first else acc_in[...]
-    copies[1].wait()
+    for copy in copies[1]:
+        copy.wait()
     for k in range(0, rows, 2):
         at = slice(k * lon, (k + 2) * lon)
         grad = dot(w_out[...], masked[:, at]) * slope[:, at]
@@ -354,11 +426,11 @@
             grid=(1,),
             in_specs=specs,
             out_specs=[full(s) for s, _ in shapes],
-            scratch_shapes=[pltpu.VMEM(x.shape, x.dtype) for x in kept]
+            scratch_shapes=[pltpu.VMEM((width, cols), BF16), pltpu.VMEM((width, cols), F32)]
             + [
                 pltpu.VMEM((3 * channels, (rows + 2) * lon), BF16),
                 pltpu.VMEM((channels, cols), BF16),
-                pltpu.SemaphoreType.DMA((2,)),
+                pltpu.SemaphoreType.DMA((2, 3)),
             ]
             + ([pltpu.VMEM(s, d) for s, d in sums] if last else []),
         ),
@@ -373,7 +445,11 @@
     rows, channels, lon = mains[0].shape
     copies = [pltpu.make_async_copy(local.at[m], out.at[m], sems.at[m]) for m in range(members)]
     for m in range(members):
-        for r, grad in enumerate(own_grads(w_conv, pres[m], z.at[m % 2], channels, rows, lon, 0)):
+        for k in range(0, rows, 2):
+            at = slice(k * lon, (k + 2) * lon)
+            z[m % 2, :, at] = dot(w_conv[...], pres[m][:, at])
+        place = {r: r for r in range(rows)}
+        for r, grad in enumerate(row_sums(z.at[m % 2], place, channels, rows, lon)):
             total = grad + total_row(r, rows, channels, cot, m, mains[m])
             if r == 0:
                 total = total + beside_low[m].astype(F32)
@@ -444,13 +520,14 @@
     low = lax.ppermute(bottom, "tile", ahead)
     high = lax.ppermute(top, "tile", behind)
     turned, column = turn(w_conv, b_conv[None, :], lon)
+    inner_pres, inner_hidden, inner_slope = inner(rounded, turned, column, w_out, cot, land)
 
     steps = [(s, s - 1) for s in range(1, leads)]
     kept = []
     mains = []
     for m in range(members):
-        main, hidden, slope = forward(m, rounded, low, high, turned, column, w_conv, w_out, cot, land)
-        kept.append((hidden, slope))
+        main, hidden, slope = forward(m, rounded, low, high, turned, column, w_conv, w_out, cot, land, inner_pres[m])
+        kept.append((inner_hidden[m], hidden, inner_slope[m], slope))
         mains.append(lax.ppermute(main, "lead", steps))
     before = []
     pres = []

time: 82.7 us -> 79 us (0.955)
  the two profiles are of different devices: /device:TPU:5 before, /device:TPU:1 now
where the time goes in v2:
time: 79 us; the launch traced here: 78.7 us
  Pallas kernels  32 us (41%)
  starting transfers between devices  24.9 us (32%)
  waiting for transfers between devices  20.3 us (26%)
  between operations  0.93 us (1%)
    pallas_call x2, Pallas kernels, weight(): pl.pallas_call(functools.partial(weight_body, member, first, last, parts)...  10.5 us
    ppermute x4, waiting for transfers between devices, exchanged(): lax.ppermute(value, 'tile', [(t, t ^ 1 << bits[t & 1]) for t in range(til...  10.5 us
    ppermute x4, starting transfers between devices, exchanged(): lax.ppermute(value, 'tile', [(t, t ^ 1 << bits[t & 1]) for t in range(til...  8.12 us
    pallas_call x2, Pallas kernels, forward(): pl.pallas_call(functools.partial(forward_body, member), grid=(1,), in_spe...  7.57 us
    pallas_call x1, Pallas kernels, inner(): pl.pallas_call(functools.partial(inner_body, members), grid=(1,), in_spec...  5.53 us
    ppermute x1, starting transfers between devices, shards(): beside_low = lax.ppermute(down, 'tile', ahead)  5.49 us
    ppermute x1, starting transfers between devices, shards(): low = lax.ppermute(bottom, 'tile', ahead)  4.65 us
    pallas_call x1, Pallas kernels, state_grad(): pl.pallas_call(functools.partial(state_body, len(pres)), grid=(1,), in_sp...  4.52 us
  transfers between devices with their start and end apart: 11, of which 7 were waited for; matrix products, arithmetic and copies ran while one was open for 0% of the time, Pallas kernels for 23%

profile of v2, /device:TPU:1, one launch (start us, length us, event | category | flops | bytes accessed | tf_op | source)
XLA Modules:
  0.0 78.7 jit_solution(3585071077766456836)
XLA Ops:
  0.7 2.8 %prep.1 = (bf16[2,8,128,128]{3,2,1,0:T(8,128)(2,1)}, bf16[2,3,128,128]{3,2,1,0:T(8,128)(2,1)}, bf16[2,3,128,128]{3,2,1,0:T(8,128)(2,1)}) custom-call(s32[2]{0:T(128)} %dates.1, s32[1]{0:T(128)} %bitcast.1.section, f32[365,128]{1,0:T(8,128)} %forcing.1, f32[2,1024,128]{2,1,0:T(8,128)} %bitcast.15, f32[2,1024,128]{2,1,0:T(8,128)} %bitcast.7, s32[8,128]{1,0:T(8,128)} %refs_4_.3), custom_call_target="tpu_custom_call" | custom-call | tf_op jit(solution)/shard_map/prep/pallas_call | solution.py:65
  3.4 4.6 %collective-permute-start = (bf16[2,3,128,128]{3,2,1,0:T(8,128)(2,1)}, bf16[2,3,128,128]{3,2,1,0:T(8,128)(2,1)S(1)}, u32[]{:S(2)}, u32[]{:S(2)}) collective-permute-start(bf16[2,3,128,128]{3,2,1,0:T(8,128)(2,1)} %get-tuple-element.44), channel_id=1, source_target_pairs={{0,1},{1,2},{2,3},{3,4},{4,5},{5,6},{6,7},{7,8},{8,9},{9,10},{10,1... | collective-permute-start | bytes 589832 | tf_op jit(solution)/shard_map/ppermute | solution.py:520
  8.1 1.9 %collective-permute-start.1 = (bf16[2,3,128,128]{3,2,1,0:T(8,128)(2,1)}, bf16[2,3,128,128]{3,2,1,0:T(8,128)(2,1)S(1)}, u32[]{:S(2)}, u32[]{:S(2)}) collective-permute-start(bf16[2,3,128,128]{3,2,1,0:T(8,128)(2,1)} %get-tuple-element.45), channel_id=1, source_target_pairs={{1,0},{2,1},{3,2},{4,3},{5,4},{6,5},{7,6},{8,7},{9,8},{10,9},{11,1... | collective-permute-start | bytes 589832 | tf_op jit(solution)/shard_map/ppermute | solution.py:521
  10.0 0.4 turn.1
  10.5 5.5 %inner.1 = (bf16[512,768]{1,0:T(8,128)(2,1)S(1)}, bf16[512,768]{1,0:T(8,128)(2,1)S(1)}, bf16[512,768]{1,0:T(8,128)(2,1)}, bf16[512,768]{1,0:T(8,128)(2,1)}, f32[512,768]{1,0:T(8,128)}, /*index=5*/f32[512,768]{1,0:T(8,128)}) custom-call(bf16[2,8,128,128]{3,2,1,0:T(8,128)(2,1)S(1)} %copy-done.2, bf16[512,1152]{1,0:T(8,128)(2,1)S(1)} %get-tuple-element.46.turned, ...), custom_call_target="tpu_custom_call" | custom-call | tf_op jit(solution)/shard_map/inner/pallas_call | solution.py:196
  16.1 0.0 collective-permute-done.low.refs_1_
  16.1 0.0 collective-permute-done.1.high.refs_2_
  16.1 3.8 %shard_map.112 = (bf16[8,128,128]{2,1,0:T(8,128)(2,1)}, bf16[512,256]{1,0:T(8,128)(2,1)}, f32[512,256]{1,0:T(8,128)}) custom-call(bf16[2,8,128,128]{3,2,1,0:T(8,128)(2,1)S(1)} %copy-done.2, bf16[2,3,128,128]{3,2,1,0:T(8,128)(2,1)S(1)} %collective-permute-done.low.refs_1_, bf16[2,3,128,128]{3,2,1,0:T(8,128)(2,1)S(1)} %collective-permute-done.1.high.refs_2_, ...), custom_call_target="tpu_custom_call" | custom-call | tf_op jit(solution)/shard_map/pallas_call | solution.py:267
  19.9 1.3 %collective-permute-start.3 = (bf16[8,128,128]{2,1,0:T(8,128)(2,1)}, bf16[8,128,128]{2,1,0:T(8,128)(2,1)S(1)}, u32[]{:S(2)}, u32[]{:S(2)}) collective-permute-start(bf16[8,128,128]{2,1,0:T(8,128)(2,1)} %get-tuple-element.55), channel_id=1, source_target_pairs={{16,0},{17,1},{18,2},{19,3},{20,4},{21,5},{22,6},{23,7},{24,8},{25... | collective-permute-start | bytes 786440 | tf_op jit(solution)/shard_map/ppermute | solution.py:531
  21.2 3.8 %shard_map.111 = (bf16[8,128,128]{2,1,0:T(8,128)(2,1)}, bf16[512,256]{1,0:T(8,128)(2,1)}, f32[512,256]{1,0:T(8,128)}) custom-call(bf16[2,8,128,128]{3,2,1,0:T(8,128)(2,1)S(1)} %copy-done.2, bf16[2,3,128,128]{3,2,1,0:T(8,128)(2,1)S(1)} %collective-permute-done.low.refs_1_, bf16[2,3,128,128]{3,2,1,0:T(8,128)(2,1)S(1)} %collective-permute-done.1.high.refs_2_, ...), custom_call_target="tpu_custom_call" | custom-call | tf_op jit(solution)/shard_map/pallas_call | solution.py:267
  25.0 1.5 %collective-permute-start.2 = (bf16[8,128,128]{2,1,0:T(8,128)(2,1)}, bf16[8,128,128]{2,1,0:T(8,128)(2,1)}, u32[]{:S(2)}, u32[]{:S(2)}) collective-permute-start(bf16[8,128,128]{2,1,0:T(8,128)(2,1)} %get-tuple-element.49), channel_id=1, source_target_pairs={{16,0},{17,1},{18,2},{19,3},{20,4},{21,5},{22,6},{23,7},{24,8},{25... | collective-permute-start | bytes 786440 | tf_op jit(solution)/shard_map/ppermute | solution.py:531
  26.5 2.2 %collective-permute-done.3.refs_7_.refs_2_ = bf16[8,128,128]{2,1,0:T(8,128)(2,1)S(1)} collective-permute-done((bf16[8,128,128]{2,1,0:T(8,128)(2,1)}, bf16[8,128,128]{2,1,0:T(8,128)(2,1)S(1)}, u32[]{:S(2)}, u32[]{:S(2)}) %collective-permute-start.3) | collective-permute-done | bytes 262176 | tf_op jit(solution)/shard_map/ppermute | solution.py:531
  28.7 4.2 %shard_map.113 = (bf16[1,128,128]{2,1,0:T(8,128)(2,1)S(1)}, bf16[1,128,128]{2,1,0:T(8,128)(2,1)S(1)}, bf16[512,1024]{1,0:T(8,128)(2,1)S(1)}, f32[1152,512]{1,0:T...) custom-call(s32[1]{0:T(128)} %bitcast.here_ref, bf16[2,8,128,128]{3,2,1,0:T(8,128)(2,1)S(1)} %copy-done.2, ...), custom_call_target="tpu_custom_call" | custom-call | tf_op jit(solution)/shard_map/pallas_call | solution.py:422
  32.9 0.6 collective-permute-done.2.refs_7_.refs_3_
  33.5 6.3 %shard_map.114 = (bf16[2,128,128]{2,1,0:T(8,128)(2,1)S(1)}, bf16[2,128,128]{2,1,0:T(8,128)(2,1)S(1)}, bf16[512,1024]{1,0:T(8,128)(2,1)S(1)}, bf16[8,88,512]{2,1,0:T(8,128)(2,1)S(1)}, f32[8,88,512]{2,1,0:T(8,128)S(1)}) custom-call(s32[1]{0:T(128)} %bitcast.here_ref, bf16[2,8,128,128]{3,2,1,0:T(8,128)(2,1)S(1)} %copy-done.2, ...), custom_call_target="tpu_custom_call" | custom-call | tf_op jit(solution)/shard_map/pallas_call | solution.py:422
  39.8 0.1 collective-permute-start.4
  39.9 2.2 %collective-permute-done.4 = bf16[8,88,512]{2,1,0:T(8,128)(2,1)S(1)} collective-permute-done((bf16[8,88,512]{2,1,0:T(8,128)(2,1)S(1)}, bf16[8,88,512]{2,1,0:T(8,128)(2,1)S(1)}, u32[]{:S(2)}, u32[]{:S(2)}) %collective-permute-start.4) | collective-permute-done | bytes 720928 | tf_op jit(solution)/shard_map/ppermute | solution.py:545
  42.1 0.2 convert_add_fusion
  42.3 4.0 %collective-permute-start.5 = (bf16[4,88,512]{2,1,0:T(8,128)(2,1)S(1)}, bf16[4,88,512]{2,1,0:T(8,128)(2,1)S(1)}, u32[]{:S(2)}, u32[]{:S(2)}) collective-permute-start(bf16[4,88,512]{2,1,0:T(8,128)(2,1)S(1)} %slice.39), channel_id=1, source_target_pairs={{0,2},{1,5},{2,0},{3,7},{4,6},{5,1},{6,4},{7,3},{8,10},{9,13},{10,... | collective-permute-start | bytes 1081352 | tf_op jit(solution)/shard_map/ppermute | solution.py:545
  46.3 5.1 %collective-permute-done.5 = bf16[4,88,512]{2,1,0:T(8,128)(2,1)S(1)} collective-permute-done((bf16[4,88,512]{2,1,0:T(8,128)(2,1)S(1)}, bf16[4,88,512]{2,1,0:T(8,128)(2,1)S(1)}, u32[]{:S(2)}, u32[]{:S(2)}) %collective-permute-start.5) | collective-permute-done | bytes 360480 | tf_op jit(solution)/shard_map/ppermute | solution.py:545
  51.4 0.1 slice_add_fusion
  51.6 1.6 %collective-permute-start.6 = (bf16[2,88,512]{2,1,0:T(8,128)(2,1)S(1)}, bf16[2,88,512]{2,1,0:T(8,128)(2,1)S(1)}, u32[]{:S(2)}, u32[]{:S(2)}) collective-permute-start(bf16[2,88,512]{2,1,0:T(8,128)(2,1)S(1)} %slice.40), channel_id=1, source_target_pairs={{0,4},{1,3},{2,6},{3,1},{4,0},{5,7},{6,2},{7,5},{8,12},{9,11},{10,... | collective-permute-start | bytes 540680 | tf_op jit(solution)/shard_map/ppermute | solution.py:545
  53.1 3.2 %collective-permute-done.6 = bf16[2,88,512]{2,1,0:T(8,128)(2,1)S(1)} collective-permute-done((bf16[2,88,512]{2,1,0:T(8,128)(2,1)S(1)}, bf16[2,88,512]{2,1,0:T(8,128)(2,1)S(1)}, u32[]{:S(2)}, u32[]{:S(2)}) %collective-permute-start.6) | collective-permute-done | bytes 180256 | tf_op jit(solution)/shard_map/ppermute | solution.py:545
  56.4 2.5 %collective-permute-start.7 = (bf16[1,88,512]{2,1,0:T(8,128)(2,1)S(1)}, bf16[1,88,512]{2,1,0:T(8,128)(2,1)S(1)}, u32[]{:S(2)}, u32[]{:S(2)}) collective-permute-start(bf16[1,88,512]{2,1,0:T(8,128)(2,1)S(1)} %slice.41), channel_id=1, source_target_pairs={{0,8},{1,9},{2,10},{3,11},{4,12},{5,13},{6,14},{7,15},{8,0},{9,1},... | collective-permute-start | bytes 270344 | tf_op jit(solution)/shard_map/ppermute | solution.py:545
  58.9 5.5 %collective-permute-start.8 = (bf16[2,128,128]{2,1,0:T(8,128)(2,1)S(1)}, bf16[2,128,128]{2,1,0:T(8,128)(2,1)S(1)}, u32[]{:S(2)}, u32[]{:S(2)}) collective-permute-start(bf16[2,128,128]{2,1,0:T(8,128)(2,1)S(1)} %get-tuple-element.73), channel_id=1, source_target_pairs={{0,1},{1,2},{2,3},{3,4},{4,5},{5,6},{6,7},{7,8},{8,9},{9,10},{10,1... | collective-permute-start | bytes 196616 | tf_op jit(solution)/shard_map/ppermute | solution.py:553
  64.4 1.9 %collective-permute-start.9 = (bf16[2,128,128]{2,1,0:T(8,128)(2,1)S(1)}, bf16[2,128,128]{2,1,0:T(8,128)(2,1)S(1)}, u32[]{:S(2)}, u32[]{:S(2)}) collective-permute-start(bf16[2,128,128]{2,1,0:T(8,128)(2,1)S(1)} %get-tuple-element.74), channel_id=1, source_target_pairs={{1,0},{2,1},{3,2},{4,3},{5,4},{6,5},{7,6},{8,7},{9,8},{10,9},{11,1... | collective-permute-start | bytes 196616 | tf_op jit(solution)/shard_map/ppermute | solution.py:554
  66.3 0.0 collective-permute-done.8.beside_low
  66.3 3.6 %collective-permute-done.9.beside_high = bf16[2,128,128]{2,1,0:T(8,128)(2,1)S(1)} collective-permute-done((bf16[2,128,128]{2,1,0:T(8,128)(2,1)S(1)}, bf16[2,128,128]{2,1,0:T(8,128)(2,1)S(1)}, u32[]{:S(2)}, u32[]{:S(2)}) %collective-permute-start.9) | collective-permute-done | bytes 65568 | tf_op jit(solution)/shard_map/ppermute | solution.py:554
  70.0 4.5 %state.1 = f32[2,1024,128]{2,1,0:T(8,128)} custom-call(bf16[1152,512]{1,0:T(8,128)(2,1)S(1)} %copy-done.1, f32[2,1024,128]{2,1,0:T(8,128)S(1)} %bitcast.13, bf16[2,128,128]{2,1,0:T(8,128)(2,1)S(1)} %collective-permute-done.8.beside_low, bf16[2,128,128]{2,1,0:T(8,128)(2,1)S(1)} %collective-permute-done.9.beside_high, ...), custom_call_target="tpu_custom_call" | custom-call | tf_op jit(solution)/shard_map/state/pallas_call | solution.py:467
  74.5 0.1 collective-permute-start.10
  74.6 3.4 %collective-permute-done.10.taken = bf16[1,88,512]{2,1,0:T(8,128)(2,1)S(1)} collective-permute-done((bf16[1,88,512]{2,1,0:T(8,128)(2,1)S(1)}, bf16[1,88,512]{2,1,0:T(8,128)(2,1)S(1)}, u32[]{:S(2)}, u32[]{:S(2)}) %collective-permute-start.10) | collective-permute-done | bytes 90144 | tf_op jit(solution)/shard_map/ppermute | solution.py:563
  78.0 0.7 finish.1
  (18 shorter events, 0.2 us)
Async XLA Ops:
  0.6 9.4 %copy-start.1 = (bf16[1152,512]{1,0:T(8,128)(2,1)S(1)}, bf16[1152,512]{1,0:T(8,128)(2,1)}, u32[]{:S(2)}) copy-start(bf16[1152,512]{1,0:T(8,128)(2,1)} %w_conv.7) | copy-start | bytes 3538948
  0.6 9.4 %copy-start.5 = (f32[512]{0:T(512)S(1)}, f32[512]{0:T(512)}, u32[]{:S(2)}) copy-start(f32[512]{0:T(512)} %param.11) | copy-start | bytes 6148
  0.7 9.8 %copy-start = (f32[1,2,128,8,128]{4,3,2,1,0:T(8,128)S(1)}, f32[1,2,128,8,128]{4,3,2,1,0:T(8,128)}, u32[]{:S(2)}) copy-start(f32[1,2,128,8,128]{4,3,2,1,0:T(8,128)} %param.9) | copy-start | bytes 3145732
  0.7 9.8 %copy-start.3 = (bf16[512,128]{1,0:T(8,128)(2,1)S(1)}, bf16[512,128]{1,0:T(8,128)(2,1)}, u32[]{:S(2)}) copy-start(bf16[512,128]{1,0:T(8,128)(2,1)} %refs_5_.3) | copy-start | bytes 393220
  0.7 9.8 %copy-start.4 = (s32[8,128]{1,0:T(8,128)S(1)}, s32[8,128]{1,0:T(8,128)}, u32[]{:S(2)}) copy-start(s32[8,128]{1,0:T(8,128)} %refs_4_.3) | copy-start | bytes 12292
  3.4 7.1 %copy-start.2 = (bf16[2,8,128,128]{3,2,1,0:T(8,128)(2,1)S(1)}, bf16[2,8,128,128]{3,2,1,0:T(8,128)(2,1)}, u32[]{:S(2)}) copy-start(bf16[2,8,128,128]{3,2,1,0:T(8,128)(2,1)} %get-tuple-element.43.rounded.refs_0_) | copy-start | bytes 1572868
  3.4 12.6 %collective-permute-start = (bf16[2,3,128,128]{3,2,1,0:T(8,128)(2,1)}, bf16[2,3,128,128]{3,2,1,0:T(8,128)(2,1)S(1)}, u32[]{:S(2)}, u32[]{:S(2)}) collective-permute-start(bf16[2,3,128,128]{3,2,1,0:T(8,128)(2,1)} %get-tuple-element.44), channel_id=1, source_target_pairs={{0,1},{1,2},{2,3},{3,4},{4,5},{5,6},{6,7},{7,8},{8,9},{9,10},{10,1... | collective-permute-start | bytes 589832 | tf_op jit(solution)/shard_map/ppermute | solution.py:520
  8.1 8.0 %collective-permute-start.1 = (bf16[2,3,128,128]{3,2,1,0:T(8,128)(2,1)}, bf16[2,3,128,128]{3,2,1,0:T(8,128)(2,1)S(1)}, u32[]{:S(2)}, u32[]{:S(2)}) collective-permute-start(bf16[2,3,128,128]{3,2,1,0:T(8,128)(2,1)} %get-tuple-element.45), channel_id=1, source_target_pairs={{1,0},{2,1},{3,2},{4,3},{5,4},{6,5},{7,6},{8,7},{9,8},{10,9},{11,1... | collective-permute-start | bytes 589832 | tf_op jit(solution)/shard_map/ppermute | solution.py:521
  19.9 8.8 %collective-permute-start.3 = (bf16[8,128,128]{2,1,0:T(8,128)(2,1)}, bf16[8,128,128]{2,1,0:T(8,128)(2,1)S(1)}, u32[]{:S(2)}, u32[]{:S(2)}) collective-permute-start(bf16[8,128,128]{2,1,0:T(8,128)(2,1)} %get-tuple-element.55), channel_id=1, source_target_pairs={{16,0},{17,1},{18,2},{19,3},{20,4},{21,5},{22,6},{23,7},{24,8},{25... | collective-permute-start | bytes 786440 | tf_op jit(solution)/shard_map/ppermute | solution.py:531
  25.0 8.5 %collective-permute-start.2 = (bf16[8,128,128]{2,1,0:T(8,128)(2,1)}, bf16[8,128,128]{2,1,0:T(8,128)(2,1)}, u32[]{:S(2)}, u32[]{:S(2)}) collective-permute-start(bf16[8,128,128]{2,1,0:T(8,128)(2,1)} %get-tuple-element.49), channel_id=1, source_target_pairs={{16,0},{17,1},{18,2},{19,3},{20,4},{21,5},{22,6},{23,7},{24,8},{25... | collective-permute-start | bytes 786440 | tf_op jit(solution)/shard_map/ppermute | solution.py:531
  39.8 2.3 %collective-permute-start.4 = (bf16[8,88,512]{2,1,0:T(8,128)(2,1)S(1)}, bf16[8,88,512]{2,1,0:T(8,128)(2,1)S(1)}, u32[]{:S(2)}, u32[]{:S(2)}) collective-permute-start(bf16[8,88,512]{2,1,0:T(8,128)(2,1)S(1)} %get-tuple-element.66), channel_id=1, source_target_pairs={{0,1},{1,0},{2,3},{3,2},{4,5},{5,4},{6,7},{7,6},{8,9},{9,8},{10,11... | collective-permute-start | bytes 2162696 | tf_op jit(solution)/shard_map/ppermute | solution.py:545
  42.3 9.1 %collective-permute-start.5 = (bf16[4,88,512]{2,1,0:T(8,128)(2,1)S(1)}, bf16[4,88,512]{2,1,0:T(8,128)(2,1)S(1)}, u32[]{:S(2)}, u32[]{:S(2)}) collective-permute-start(bf16[4,88,512]{2,1,0:T(8,128)(2,1)S(1)} %slice.39), channel_id=1, source_target_pairs={{0,2},{1,5},{2,0},{3,7},{4,6},{5,1},{6,4},{7,3},{8,10},{9,13},{10,... | collective-permute-start | bytes 1081352 | tf_op jit(solution)/shard_map/ppermute | solution.py:545
  51.6 4.8 %collective-permute-start.6 = (bf16[2,88,512]{2,1,0:T(8,128)(2,1)S(1)}, bf16[2,88,512]{2,1,0:T(8,128)(2,1)S(1)}, u32[]{:S(2)}, u32[]{:S(2)}) collective-permute-start(bf16[2,88,512]{2,1,0:T(8,128)(2,1)S(1)} %slice.40), channel_id=1, source_target_pairs={{0,4},{1,3},{2,6},{3,1},{4,0},{5,7},{6,2},{7,5},{8,12},{9,11},{10,... | collective-permute-start | bytes 540680 | tf_op jit(solution)/shard_map/ppermute | solution.py:545
  56.4 18.1 %collective-permute-start.7 = (bf16[1,88,512]{2,1,0:T(8,128)(2,1)S(1)}, bf16[1,88,512]{2,1,0:T(8,128)(2,1)S(1)}, u32[]{:S(2)}, u32[]{:S(2)}) collective-permute-start(bf16[1,88,512]{2,1,0:T(8,128)(2,1)S(1)} %slice.41), channel_id=1, source_target_pairs={{0,8},{1,9},{2,10},{3,11},{4,12},{5,13},{6,14},{7,15},{8,0},{9,1},... | collective-permute-start | bytes 270344 | tf_op jit(solution)/shard_map/ppermute | solution.py:545
  58.9 7.4 %collective-permute-start.8 = (bf16[2,128,128]{2,1,0:T(8,128)(2,1)S(1)}, bf16[2,128,128]{2,1,0:T(8,128)(2,1)S(1)}, u32[]{:S(2)}, u32[]{:S(2)}) collective-permute-start(bf16[2,128,128]{2,1,0:T(8,128)(2,1)S(1)} %get-tuple-element.73), channel_id=1, source_target_pairs={{0,1},{1,2},{2,3},{3,4},{4,5},{5,6},{6,7},{7,8},{8,9},{9,10},{10,1... | collective-permute-start | bytes 196616 | tf_op jit(solution)/shard_map/ppermute | solution.py:553
  64.4 5.6 %collective-permute-start.9 = (bf16[2,128,128]{2,1,0:T(8,128)(2,1)S(1)}, bf16[2,128,128]{2,1,0:T(8,128)(2,1)S(1)}, u32[]{:S(2)}, u32[]{:S(2)}) collective-permute-start(bf16[2,128,128]{2,1,0:T(8,128)(2,1)S(1)} %get-tuple-element.74), channel_id=1, source_target_pairs={{1,0},{2,1},{3,2},{4,3},{5,4},{6,5},{7,6},{8,7},{9,8},{10,9},{11,1... | collective-permute-start | bytes 196616 | tf_op jit(solution)/shard_map/ppermute | solution.py:554
  74.5 3.4 %collective-permute-start.10 = (bf16[1,88,512]{2,1,0:T(8,128)(2,1)S(1)}, bf16[1,88,512]{2,1,0:T(8,128)(2,1)S(1)}, u32[]{:S(2)}, u32[]{:S(2)}) collective-permute-start(bf16[1,88,512]{2,1,0:T(8,128)(2,1)S(1)} %get-tuple-element.82), channel_id=1, source_target_pairs={{0,16},{16,0},{1,17},{17,1},{2,18},{18,2},{3,19},{19,3},{4,20},{20... | collective-permute-start | bytes 270344 | tf_op jit(solution)/shard_map/ppermute | solution.py:563
